TPU v7x, 32 devices: a whole 2x2x4 slice. The times are simulated.
32 devices in a mesh: half: 2 (over y), row: 4 (over z), col: 4 (over x, core).
Axes of the slice: x: 2, y: 2, z: 4, core: 2. Of those that a mesh axis runs over, the one named last changes fastest.
Arguments:
- front_init: float32 [10240, 10240], P(('half', 'row'), 'col'), may hold values from -2 to 8, as said below
- child_update: float32 [2, 8192, 8192], P('half', 'row', 'col'), may hold values from -2 to 8, as said below
- child_map: int32 [2, 8192], replicated, may hold values from 0 to 10239, as said below
Outputs:
- factor_front: float32 [10240, 10240], P(('half', 'row'), 'col')
Inputs may be any that keep to these rules, and one draw needn't show every extreme that they name: `child_map`: each child's entries are distinct. Each aligned block of 128 child indices maps onto one whole block of 128 front indices; write b(j) for the front block of child block j. For every r and q below 4, exactly 4 child blocks j with j % 4 == r have b(j) % 4 == q, and these share one value of b(j) % 8. Symmetric in natural order, and front_init minus the identity is positive semidefinite. `child_update`: each child's matrix is symmetric positive semidefinite.
All inputs are finite; a program needn't handle non-finite values.
Results may differ from a plain program's by a relative error of at most 0.0001.
Values sent between devices are 32-bit elements; how exact they have to be, the bound alone decides.
A program may use at most 256 MiB of HBM per device.

v0:
```python
import jax
import jax.numpy as jnp
from jax import lax
from jax.sharding import PartitionSpec as P

BLOCK_EDGE = 128
PANELS = 2
PANEL = 256


def column_order(which_map, source, grid_size, blocks_dev, slot_count):
    local_ids = jnp.arange(blocks_dev)
    targets = which_map[local_ids * grid_size + source] % grid_size
    return jnp.argsort(targets * blocks_dev + local_ids).reshape(grid_size, slot_count)


def row_slots(which_map, source, grid_size, group_count, blocks_dev, slot_count):
    local_ids = jnp.arange(blocks_dev)
    targets = which_map[local_ids * grid_size + source] % group_count
    onehot = targets[None, :] == jnp.arange(group_count)[:, None]
    ranking = jnp.cumsum(onehot.astype(jnp.int32), axis=1)
    matches = onehot[:, None, :] & (
        ranking[:, None, :] == jnp.arange(1, slot_count + 1)[None, :, None]
    )
    slot_index = jnp.sum(matches.astype(jnp.int32) * local_ids[None, None, :], axis=2)
    filled = jnp.any(matches, axis=2)
    return (slot_index, filled)


def on_device(front_init, child_update, child_map):
    grid_size = lax.axis_size("row")
    halves = lax.axis_size("half")
    group_count = halves * grid_size
    my_child = lax.axis_index("half")
    my_row = lax.axis_index("row")
    my_col = lax.axis_index("col")
    my_group = lax.axis_index(("half", "row"))
    child_rows = child_update.shape[1]
    blocks_dev = child_rows // BLOCK_EDGE
    slot_count = blocks_dev // grid_size
    front_rows, front_cols = front_init.shape
    row_blocks = front_rows // BLOCK_EDGE
    block_map = child_map.reshape(2, -1, BLOCK_EDGE)[:, :, 0] // BLOCK_EDGE
    inner_perm = child_map.reshape(2, -1, BLOCK_EDGE) % BLOCK_EDGE
    own_map = block_map[my_child]
    send_order = column_order(own_map, my_col, grid_size, blocks_dev, slot_count).reshape(-1)
    blocks = child_update[0].reshape(child_rows, blocks_dev, BLOCK_EDGE)
    outgoing = jnp.take(blocks, send_order, axis=1).reshape(child_rows, blocks_dev * BLOCK_EDGE)
    incoming = lax.all_to_all(outgoing, "col", split_axis=1, concat_axis=1, tiled=True)
    slot_index, filled = row_slots(own_map, my_row, grid_size, group_count, blocks_dev, slot_count)
    stacked = incoming.reshape(blocks_dev, BLOCK_EDGE, -1)
    packed = jnp.take(stacked, slot_index.reshape(-1), axis=0).reshape(
        group_count, slot_count, BLOCK_EDGE, -1
    )
    packed = jnp.where(filled[:, :, None, None], packed, 0.0).reshape(
        group_count * slot_count * BLOCK_EDGE, -1
    )
    arrived = lax.all_to_all(packed, ("half", "row"), split_axis=0, concat_axis=0, tiled=True)
    arrived = arrived.reshape(halves, grid_size * slot_count * BLOCK_EDGE, -1)
    front_local = front_init
    sources = jnp.arange(grid_size)
    for which_child in range(2):
        which_map = block_map[which_child]
        which_inner = inner_perm[which_child]
        orders = jax.vmap(
            lambda source: column_order(which_map, source, grid_size, blocks_dev, slot_count)
        )(sources)
        col_blocks = (orders[:, my_col, :] * grid_size + sources[:, None]).reshape(-1)
        col_index = (
            (which_map[col_blocks] // grid_size * BLOCK_EDGE)[:, None] + which_inner[col_blocks]
        ).reshape(-1)
        slot_all, fill_all = jax.vmap(
            lambda source: row_slots(
                which_map, source, grid_size, group_count, blocks_dev, slot_count
            )
        )(sources)
        mine_slot = slot_all[:, my_group, :]
        mine_fill = fill_all[:, my_group, :]
        child_blocks = mine_slot * grid_size + sources[:, None]
        target_blocks = which_map[child_blocks]
        row_index = (target_blocks // group_count * BLOCK_EDGE)[:, :, None] + which_inner[
            child_blocks
        ]
        row_index = jnp.where(mine_fill[:, :, None], row_index, front_rows).reshape(-1)
        spread = (
            jnp.zeros((arrived.shape[1], front_cols), jnp.float32)
            .at[:, col_index]
            .set(arrived[which_child])
        )
        front_local = front_local.at[row_index].add(spread, mode="drop")
    row_ids = jnp.arange(front_rows)
    natural_rows = (
        row_ids // BLOCK_EDGE * group_count + my_group
    ) * BLOCK_EDGE + row_ids % BLOCK_EDGE
    col_ids = jnp.arange(front_cols)
    natural_cols = (col_ids // BLOCK_EDGE * grid_size + my_col) * BLOCK_EDGE + col_ids % BLOCK_EDGE
    identity = jnp.eye(PANEL, dtype=jnp.float32)
    for panel_index in range(PANELS):
        panel_start = panel_index * PANEL
        panel_end = panel_start + PANEL
        panel_slab = lax.all_gather(front_local[:, :BLOCK_EDGE], "col", axis=1, tiled=True)[
            :, panel_start:panel_end
        ]
        pieces = []
        for block_part in range(PANEL // BLOCK_EDGE):
            owner_group = (panel_start // BLOCK_EDGE + block_part) % group_count
            pieces.append(jnp.where(my_group == owner_group, panel_slab[:BLOCK_EDGE], 0.0))
        diagonal = lax.psum(jnp.concatenate(pieces, axis=0), ("half", "row"))
        factor = jnp.linalg.cholesky(diagonal)
        inverse = lax.linalg.triangular_solve(factor, identity, left_side=True, lower=True)
        panel_rows = jnp.dot(panel_slab, inverse.T, precision=lax.Precision.HIGHEST)
        panel_rows = jnp.where((natural_rows >= panel_start)[:, None], panel_rows, 0.0)
        everything = lax.all_gather(panel_rows, ("half", "row"), axis=0, tiled=True)
        everything = everything.reshape(halves, grid_size, row_blocks, BLOCK_EDGE, PANEL)
        selected = lax.dynamic_index_in_dim(everything, my_col, axis=1, keepdims=False)
        column_panel = selected.transpose(1, 0, 2, 3).reshape(front_cols, PANEL)
        update = jnp.dot(panel_rows, column_panel.T, precision=lax.Precision.HIGHEST)
        trailing = (natural_rows >= panel_end)[:, None] & (natural_cols >= panel_end)[None, :]
        front_local = jnp.where(trailing, front_local - update, front_local)
        in_panel = (natural_cols >= panel_start) & (natural_cols < panel_end)
        panel_values = jnp.take(
            panel_rows, jnp.clip(natural_cols - panel_start, 0, PANEL - 1), axis=1
        )
        front_local = jnp.where(in_panel[None, :], panel_values, front_local)
        upper_zero = ((natural_rows >= panel_start) & (natural_rows < panel_end))[:, None] & (
            natural_cols >= panel_end
        )[None, :]
        front_local = jnp.where(upper_zero, 0.0, front_local)
    return front_local


def solution(mesh):
    placed = (P(("half", "row"), "col"), P("half", "row", "col"), P())
    return jax.shard_map(
        on_device, mesh=mesh, in_specs=placed, out_specs=P(("half", "row"), "col"), check_vma=False
    )
```

profile of v0, /device:TPU:18, one launch (start us, length us, event | category | flops | bytes accessed | tf_op | source)
XLA Modules:
  0.0 2030.9 jit_solution(14741416370974196072)
XLA Ops:
  20.2 17.6 copy.111
  37.8 17.6 copy.112
  55.4 13.8 gather_fusion.7
  69.2 17.6 copy.113
  106.8 180.5 %all-to-all-done = f32[2048,4,512]{0,2,1:T(8,128)} async-done(((f32[2048,4,512]{0,2,1:T(8,128)}), f32[2048,4,512]{0,2,1:T(8,128)}, u32[]{:S(2)}, u32[]{:S(2)}) %all-to-all-start) | async-done | bytes 16777248 | tf_op jit(solution)/shard_map/all_to_all | solution.py:49
  287.3 14.1 copy.151
  301.4 18.0 copy.142
  319.4 18.8 gather_fusion.8
  338.2 23.1 %fusion = f32[8,512,2048]{2,1,0:T(8,128)} fusion(pred[8,512]{1,0:T(8,128)(4,1)S(1)} %broadcast_bitcast_fusion, pred[8,512]{1,0:T(8,128)(4,1)S(1)} %broadcast_bitcast_fusion.1, f32[8,512,2048]{2,1,0:T(8,128)} %bitcast.166), kind=kLoop, calls=%fused_computation.25 | loop fusion | flops 16777216 | bytes 67117056 | tf_op jit(solution)/shard_map/jit(_where)/select_n | solution.py:55
  383.2 704.7 %all-to-all-done.1 = f32[8,512,2048]{2,1,0:T(8,128)} async-done(((f32[8,512,2048]{2,1,0:T(8,128)}), f32[8,512,2048]{2,1,0:T(8,128)}, u32[]{:S(2)}, u32[]{:S(2)}) %all-to-all-start.1) | async-done | bytes 33554464 | tf_op jit(solution)/shard_map/all_to_all | solution.py:58
  1088.0 21.1 %fusion.91 = (f32[4,512,2048]{2,1,0:T(8,128)}, f32[4,512,2048]{2,1,0:T(8,128)}) fusion(f32[8,512,2048]{2,1,0:T(8,128)} %all-to-all-done.1), kind=kLoop, calls=%fused_computation.286 | loop fusion | bytes 67108864 | tf_op jit(solution)/shard_map/slice | solution.py:88
  1109.1 17.6 copy.143
  1126.7 21.8 %scatter_custom_fusion = f32[2048,2560]{0,1:T(8,128)} fusion(s32[2048]{0:T(1024)S(1)} %bitcast.190, f32[2048,2048]{0,1:T(8,128)} %copy.143, f32[]{:T(128)} %constant.323.clone.1), kind=kCustom, calls=%fused_computation.30 | custom fusion | bytes 37748740 | tf_op jit(solution)/shard_map/scatter | solution.py:88
  1148.5 20.0 copy.117
  1168.5 17.6 copy.146
  1186.1 21.9 %scatter_custom_fusion.2 = f32[2048,2560]{0,1:T(8,128)} fusion(s32[2048]{0:T(1024)S(1)} %bitcast.189, f32[2048,2048]{0,1:T(8,128)} %copy.146, f32[]{:T(128)} %constant.323.clone.1), kind=kCustom, calls=%fused_computation.28 | custom fusion | bytes 37748740 | tf_op jit(solution)/shard_map/scatter | solution.py:88
  1207.9 19.9 copy.125
  1227.9 42.7 %scatter_fusion = f32[1280,2560]{1,0:T(8,128)} fusion(f32[1280,2560]{1,0:T(8,128)} %copy.186, s32[2048]{0:T(1024)S(1)} %bitcast.180, f32[2048,2560]{1,0:T(8,128)} %copy.117), kind=kCustom, calls=%fused_computation.17 | custom fusion | flops 5242880 | bytes 62922752 | tf_op jit(solution)/shard_map/scatter-add | solution.py:90
  1270.6 42.5 %scatter_fusion.1 = f32[1280,2560]{1,0:T(8,128)} fusion(f32[1280,2560]{1,0:T(8,128)} %scatter_fusion, s32[2048]{0:T(1024)S(1)} %bitcast.181, f32[2048,2560]{1,0:T(8,128)} %copy.125), kind=kCustom, calls=%fused_computation.19 | custom fusion | flops 5242880 | bytes 62922752 | tf_op jit(solution)/shard_map/scatter-add | solution.py:90
  1313.0 14.0 copy.126
  1329.1 25.7 %all-gather.5.cloned.1.call-done = f32[1280,512]{0,1:T(8,128)} async-done(((f32[1280,128]{0,1:T(8,128)}), f32[1280,512]{0,1:T(8,128)}) %all-gather.5.cloned.1.call-update) | async-done | bytes 2621456 | tf_op jit(solution)/shard_map/all_gather | solution.py:101
  1357.0 71.8 %all-reduce.4.cloned.1.call-done = f32[256,256]{0,1:T(8,128)} async-done(((f32[256,256]{0,1:T(8,128)}), f32[256,256]{0,1:T(8,128)}) %all-reduce.4.cloned.1.call-update) | async-done | bytes 262160 | tf_op jit(solution)/shard_map/psum | solution.py:108
  1453.0 11.7 cholesky.147
  1471.6 19.7 custom-call.14
  1508.5 138.6 %all-gather.7.cloned.1.call-done = f32[10240,256]{1,0:T(8,128)} async-done(((f32[1280,256]{1,0:T(8,128)}), f32[10240,256]{1,0:T(8,128)}) %all-gather.7.cloned.1.call-update) | async-done | bytes 10485776 | tf_op jit(solution)/shard_map/all_gather | solution.py:113
  1649.4 19.9 fusion.6
  1671.3 23.8 %all-gather.9.cloned.1.call-done = f32[1280,512]{0,1:T(8,128)} async-done(((f32[1280,128]{0,1:T(8,128)}), f32[1280,512]{0,1:T(8,128)}) %all-gather.9.cloned.1.call-update) | async-done | bytes 2621456 | tf_op jit(solution)/shard_map/all_gather | solution.py:101
  1697.1 72.3 %all-reduce.6.cloned.1.call-done = f32[256,256]{0,1:T(8,128)} async-done(((f32[256,256]{0,1:T(8,128)}), f32[256,256]{0,1:T(8,128)}) %all-reduce.6.cloned.1.call-update) | async-done | bytes 262160 | tf_op jit(solution)/shard_map/psum | solution.py:108
  1812.2 19.7 custom-call.16
  1849.2 138.4 %all-gather.11.cloned.1.call-done = f32[10240,256]{1,0:T(8,128)} async-done(((f32[1280,256]{1,0:T(8,128)}), f32[10240,256]{1,0:T(8,128)}) %all-gather.11.cloned.1.call-update) | async-done | bytes 10485776 | tf_op jit(solution)/shard_map/all_gather | solution.py:113
  1989.9 19.9 fusion.8
  2009.8 13.9 copy.137
  (202 shorter events, 181.3 us)
Async XLA Ops:
  6.5 10.8 copy-start.2
  98.4 188.9 %all-to-all-start = ((f32[2048,4,512]{0,2,1:T(8,128)}), f32[2048,4,512]{0,2,1:T(8,128)}, u32[]{:S(2)}, u32[]{:S(2)}) async-start(f32[2048,4,512]{0,2,1:T(8,128)} %bitcast_select_fusion.1), calls=%async_computation | async-start | bytes 33554432 | tf_op jit(solution)/shard_map/all_to_all | solution.py:49
  361.3 726.7 %all-to-all-start.1 = ((f32[8,512,2048]{2,1,0:T(8,128)}), f32[8,512,2048]{2,1,0:T(8,128)}, u32[]{:S(2)}, u32[]{:S(2)}) async-start(f32[8,512,2048]{2,1,0:T(8,128)} %fusion), calls=%async_computation.1 | async-start | bytes 67108864 | tf_op jit(solution)/shard_map/all_to_all | solution.py:58
  368.4 986.4 %all-gather.5.cloned.1.call-start = ((), (), s32[]{:S(2)}) async-start(), calls=%async_computation.2 | async-start | bytes 3276800 | tf_op jit(solution)/shard_map/all_gather | solution.py:101
  1227.9 42.7 %copy-start.3 = (s32[2048,1]{0,1:T(1,128)S(1)}, s32[2048,1]{0,1:T(1,128)}, u32[]{:S(2)}) copy-start(s32[2048,1]{0,1:T(1,128)} %compare_select_fusion.1) | copy-start | bytes 24580
  1329.0 99.9 %all-reduce.4.cloned.1.call-start = ((), (), s32[]{:S(2)}) async-start(), calls=%async_computation.3 | async-start | bytes 524288 | tf_op jit(solution)/shard_map/psum | solution.py:108
  1356.5 290.6 %all-gather.7.cloned.1.call-start = ((), (), s32[]{:S(2)}) async-start(), calls=%async_computation.4 | async-start | bytes 11796480 | tf_op jit(solution)/shard_map/all_gather | solution.py:113
  1496.9 198.2 %all-gather.9.cloned.1.call-start = ((), (), s32[]{:S(2)}) async-start(), calls=%async_computation.5 | async-start | bytes 3276800 | tf_op jit(solution)/shard_map/all_gather | solution.py:101
  1498.8 150.5 %copy-start.1 = (f32[1280,256]{1,0:T(8,128)S(1)}, f32[1280,256]{1,0:T(8,128)}, u32[]{:S(2)}) copy-start(f32[1280,256]{1,0:T(8,128)} %convolution_select_fusion.1) | copy-start | bytes 3932164
  1671.2 98.2 %all-reduce.6.cloned.1.call-start = ((), (), s32[]{:S(2)}) async-start(), calls=%async_computation.6 | async-start | bytes 524288 | tf_op jit(solution)/shard_map/psum | solution.py:108
  1696.8 290.8 %all-gather.11.cloned.1.call-start = ((), (), s32[]{:S(2)}) async-start(), calls=%async_computation.7 | async-start | bytes 11796480 | tf_op jit(solution)/shard_map/all_gather | solution.py:113
  1839.3 150.6 %copy-start = (f32[1280,256]{1,0:T(8,128)S(1)}, f32[1280,256]{1,0:T(8,128)}, u32[]{:S(2)}) copy-start(f32[1280,256]{1,0:T(8,128)} %convolution_select_fusion) | copy-start | bytes 3932164
Sparse Core Ops, SparseCore 0:
  1329.1 25.6 all-gather.4
  1358.1 70.6 all-reduce.3
  1497.1 149.9 all-gather.6
  1671.3 23.7 all-gather.8
  1698.7 70.6 all-reduce.5
  1837.6 149.9 all-gather.10
where the time goes:
time: 2040 us; the launch traced here: 2030 us
  waiting for transfers between devices  1360 us (67%)
  local copies, waits for them, and re-layouts  348 us (17%)
  other arithmetic  242 us (12%)
  matrix products  51.8 us (3%)
    all_to_all x1, waiting for transfers between devices, on_device(): lax.all_to_all(packed, ('half', 'row'), split_axis=0, concat_axis=0, tile...  705 us
    all_gather x2, waiting for transfers between devices, on_device(): everything = lax.all_gather(panel_rows, ('half', 'row'), axis=0, tiled=True)  277 us
    all_to_all x1, waiting for transfers between devices, on_device(): lax.all_to_all(outgoing, 'col', split_axis=1, concat_axis=1, tiled=True)  180 us
    psum x2, waiting for transfers between devices, on_device(): diagonal = lax.psum(jnp.concatenate(pieces, axis=0), ('half', 'row'))  144 us
    scatter-add x2, other arithmetic, on_device(): front_local = front_local.at[row_index].add(spread, mode='drop')  85.1 us
    scatter x4, local copies, waits for them, and re-layouts, on_device(): spread = jnp.zeros((arrived.shape[1], front_cols), jnp.float32).at[:, col...  83.5 us
    another operation x14, other arithmetic, on_device(): factor = jnp.linalg.cholesky(diagonal)  69.3 us
    slice x3, local copies, waits for them, and re-layouts, on_device(): arrived[which_child]  56.4 us
  transfers between devices with their start and end apart: 8, of which 8 were waited for; matrix products, arithmetic and copies ran while one was open for 2% of the time, Pallas kernels for 0%

commit v1 on v0

v1 whole, which is shorter than its diff:
```python
import functools

import jax
import jax.numpy as jnp
from jax import lax
from jax.experimental import pallas as pl
from jax.experimental.pallas import tpu as pltpu
from jax.sharding import PartitionSpec as P

BE = 128
PANEL = 256
WIDE = 512
HIGHEST = lax.Precision.HIGHEST
F32 = jnp.float32
BF16 = jnp.bfloat16


def absdiff(a, b):
    return jnp.maximum(a - b, b - a)


def use_direct(a, b, x, y):
    direct = 2 * absdiff(a, x) + absdiff(b // 2, y // 2)
    swapped = 2 * absdiff(b, x) + absdiff(a // 2, y // 2)
    return direct <= swapped


def pack_kernel(grid_size, slots, row_order, col_order, src, dst):
    for y in range(grid_size):
        for k in range(slots):
            at = pl.multiple_of(col_order[y * slots + k] * BE, BE)
            dst[0, y, :, k * BE : (k + 1) * BE] = src[:, pl.ds(at, BE)]


def pack(child, row_order, col_order, grid_size, slots):
    rows, cols = child.shape
    side = slots * BE
    return pl.pallas_call(
        functools.partial(pack_kernel, grid_size, slots),
        grid_spec=pltpu.PrefetchScalarGridSpec(
            num_scalar_prefetch=2,
            grid=(grid_size * slots,),
            in_specs=[pl.BlockSpec((BE, cols), lambda n, ro, co: (ro[n], 0))],
            out_specs=pl.BlockSpec(
                (1, grid_size, BE, side), lambda n, ro, co: (n // slots, 0, n % slots, 0)
            ),
        ),
        out_shape=jax.ShapeDtypeStruct((grid_size, grid_size, side, side), F32),
    )(row_order, col_order, child)


def exchange_kernel(grid_size, src, dst, send_direct, send_swap, recv, local):
    r = lax.axis_index("row")
    s = lax.axis_index("col")
    half = lax.axis_index("half")
    g = grid_size

    def peer(k):
        return (r + k // g) % g, (s + k % g) % g

    barrier = pltpu.get_barrier_semaphore()

    def greet(k, carry):
        x, y = peer(k)
        pl.semaphore_signal(
            barrier, inc=1, device_id=(half, x, y), device_id_type=pl.DeviceIdType.MESH
        )
        return carry

    lax.fori_loop(1, g * g, greet, 0)
    pl.semaphore_wait(barrier, g * g - 1)

    own = pltpu.make_async_copy(src.at[r, s], dst.at[r, s], local.at[0])
    own_swap = pltpu.make_async_copy(src.at[s, r], dst.at[s, r], local.at[1])
    own.start()

    @pl.when(r != s)
    def _():
        own_swap.start()

    def direct_copy(k, x, y):
        return pltpu.make_async_remote_copy(
            src_ref=src.at[x, y],
            dst_ref=dst.at[r, s],
            send_sem=send_direct.at[k],
            recv_sem=recv.at[r * g + s],
            device_id=(half, x, y),
            device_id_type=pl.DeviceIdType.MESH,
        )

    def swap_copy(k, x, y):
        return pltpu.make_async_remote_copy(
            src_ref=src.at[y, x],
            dst_ref=dst.at[s, r],
            send_sem=send_swap.at[k],
            recv_sem=recv.at[s * g + r],
            device_id=(half, x, y),
            device_id_type=pl.DeviceIdType.MESH,
        )

    def send(k, carry):
        x, y = peer(k)

        @pl.when(use_direct(r, s, x, y))
        def _():
            direct_copy(k, x, y).start()

        @pl.when(jnp.logical_not(use_direct(s, r, x, y)))
        def _():
            swap_copy(k, x, y).start()

        return carry

    lax.fori_loop(1, g * g, send, 0)

    def sent(k, carry):
        x, y = peer(k)

        @pl.when(use_direct(r, s, x, y))
        def _():
            direct_copy(k, x, y).wait_send()

        @pl.when(jnp.logical_not(use_direct(s, r, x, y)))
        def _():
            swap_copy(k, x, y).wait_send()

        return carry

    lax.fori_loop(1, g * g, sent, 0)

    def arrived(k, carry):
        a = k // g
        b = k % g
        mine = jnp.logical_or(
            jnp.logical_and(a == r, b == s), jnp.logical_and(a == s, b == r)
        )

        @pl.when(jnp.logical_not(mine))
        def _():
            pltpu.make_async_remote_copy(
                src_ref=src.at[a, b],
                dst_ref=dst.at[a, b],
                send_sem=send_direct.at[0],
                recv_sem=recv.at[k],
                device_id=(half, (r + 1) % g, s),
                device_id_type=pl.DeviceIdType.MESH,
            ).wait_recv()

        return carry

    lax.fori_loop(0, g * g, arrived, 0)
    own.wait()

    @pl.when(r != s)
    def _():
        own_swap.wait()


def exchange(packed, grid_size):
    n = grid_size * grid_size
    return pl.pallas_call(
        functools.partial(exchange_kernel, grid_size),
        out_shape=jax.ShapeDtypeStruct(packed.shape, F32),
        in_specs=[pl.BlockSpec(memory_space=pl.ANY)],
        out_specs=pl.BlockSpec(memory_space=pl.ANY),
        scratch_shapes=[
            pltpu.SemaphoreType.DMA((n,)),
            pltpu.SemaphoreType.DMA((n,)),
            pltpu.SemaphoreType.DMA((n,)),
            pltpu.SemaphoreType.DMA((2,)),
        ],
        compiler_params=pltpu.CompilerParams(collective_id=0, has_side_effects=True),
    )(packed)


def place_kernel(
    grid_size, slots, steps, chunk_at, t_at, u_at, swapped, valid,
    front, chunk, row_perm, col_perm, out, acc, work, mid, sem,
):
    n = pl.program_id(0)
    a = n // grid_size
    s = n % grid_size

    @pl.when(n == 0)
    def _():
        load = pltpu.make_async_copy(front, acc, sem)
        load.start()
        load.wait()

    @pl.when(valid[a] == 1)
    def _():
        @pl.when(swapped[n] == 1)
        def _():
            work[...] = chunk[0].T

        @pl.when(swapped[n] == 0)
        def _():
            work[...] = chunk[0]

        for i in range(slots):
            t = pl.multiple_of(t_at[a * slots + i] * BE, BE)
            part = work[i * BE : (i + 1) * BE, :]
            high = part.astype(BF16)
            low = (part - high.astype(F32)).astype(BF16)
            perm = row_perm[0, i]
            mid[0] = jnp.dot(perm, high, preferred_element_type=F32).astype(BF16)
            mid[1] = jnp.dot(perm, low, preferred_element_type=F32).astype(BF16)
            for k in range(slots):
                u = pl.multiple_of(u_at[s * slots + k] * BE, BE)
                lanes = slice(k * BE, (k + 1) * BE)
                both = jnp.concatenate([mid[0, :, lanes], mid[1, :, lanes]], axis=1)
                perm2 = jnp.concatenate([col_perm[0, k], col_perm[0, k]], axis=0)
                acc[pl.ds(t, BE), pl.ds(u, BE)] += jnp.dot(
                    both, perm2, preferred_element_type=F32
                )

    @pl.when(n == steps - 1)
    def _():
        store = pltpu.make_async_copy(acc, out, sem)
        store.start()
        store.wait()


def place(front, chunks, chunk_at, t_at, u_at, swapped, valid, row_perm, col_perm, grid_size):
    slots = row_perm.shape[1]
    steps = row_perm.shape[0] * grid_size
    side = slots * BE
    return pl.pallas_call(
        functools.partial(place_kernel, grid_size, slots, steps),
        grid_spec=pltpu.PrefetchScalarGridSpec(
            num_scalar_prefetch=5,
            grid=(steps,),
            in_specs=[
                pl.BlockSpec(memory_space=pl.ANY),
                pl.BlockSpec((1, side, side), lambda n, ca, *_: (ca[n], 0, 0)),
                pl.BlockSpec((1, slots, BE, BE), lambda n, *_: (n // grid_size, 0, 0, 0)),
                pl.BlockSpec((1, slots, BE, BE), lambda n, *_: (n % grid_size, 0, 0, 0)),
            ],
            out_specs=pl.BlockSpec(memory_space=pl.ANY),
            scratch_shapes=[
                pltpu.VMEM(front.shape, F32),
                pltpu.VMEM((side, side), F32),
                pltpu.VMEM((2, BE, side), BF16),
                pltpu.SemaphoreType.DMA,
            ],
        ),
        out_shape=jax.ShapeDtypeStruct(front.shape, F32),
        compiler_params=pltpu.CompilerParams(vmem_limit_bytes=40 * 1024 * 1024),
        cost_estimate=pl.CostEstimate(
            flops=4_000_000_000, bytes_accessed=36_000_000, transcendentals=0
        ),
    )(chunk_at, t_at, u_at, swapped, valid, front, chunks, row_perm, col_perm)


def update_kernel(place_of, front, lrow, lcol, out, col_high, col_low):
    t = pl.program_id(0)
    dims = (((1,), (1,)), ((), ()))

    @pl.when(t == 0)
    def _():
        whole = lcol[...]
        high = whole.astype(BF16)
        col_high[...] = high
        col_low[...] = (whole - high.astype(F32)).astype(BF16)

    rows = lrow[...]
    high = rows.astype(BF16)
    low = (rows - high.astype(F32)).astype(BF16)
    group = place_of[0]
    col = place_of[1]
    panel_row = jnp.logical_and(t == 0, group < WIDE // BE)
    width = out.shape[1]
    step = WIDE if width % WIDE == 0 else 2 * BE
    for at in range(0, width, step):
        cols = slice(at, at + step)
        ch = col_high[cols, :]
        cl = col_low[cols, :]
        total = lax.dot_general(high, ch, dims, preferred_element_type=F32)
        total += lax.dot_general(high, cl, dims, preferred_element_type=F32)
        total += lax.dot_general(low, ch, dims, preferred_element_type=F32)
        value = front[:, cols] - total
        out[:, cols] = jnp.where(panel_row, 0.0, value)

    @pl.when(col < WIDE // BE)
    def _():
        at = pl.multiple_of(jnp.minimum(col, WIDE // BE - 1) * BE, BE)
        out[:, :BE] = lrow[:, pl.ds(at, BE)]


def update(front, lrow, lcol, place_of):
    rows, cols = front.shape
    return pl.pallas_call(
        update_kernel,
        grid_spec=pltpu.PrefetchScalarGridSpec(
            num_scalar_prefetch=1,
            grid=(rows // BE,),
            in_specs=[
                pl.BlockSpec((BE, cols), lambda t, *_: (t, 0)),
                pl.BlockSpec((BE, WIDE), lambda t, *_: (t, 0)),
                pl.BlockSpec((cols, WIDE), lambda t, *_: (0, 0)),
            ],
            out_specs=pl.BlockSpec((BE, cols), lambda t, *_: (t, 0)),
            scratch_shapes=[pltpu.VMEM((cols, WIDE), BF16), pltpu.VMEM((cols, WIDE), BF16)],
        ),
        out_shape=jax.ShapeDtypeStruct(front.shape, F32),
        compiler_params=pltpu.CompilerParams(vmem_limit_bytes=48 * 1024 * 1024),
        cost_estimate=pl.CostEstimate(
            flops=10_000_000_000, bytes_accessed=34_000_000, transcendentals=0
        ),
    )(place_of, front, lrow, lcol)


def child_tables(which_map, which_inner, grid_size, group_count, my_row, my_col, my_half, cap, slots):
    blocks_dev = slots * grid_size
    local_ids = jnp.arange(blocks_dev)
    residues = jnp.arange(grid_size)
    ids = local_ids[None, :] * grid_size + residues[:, None]
    targets = which_map[ids] % grid_size
    order = jnp.argsort(targets * blocks_dev + local_ids[None, :], axis=1)
    order = order.reshape(grid_size, grid_size, slots)
    row_ids = order[:, my_row, :] * grid_size + residues[:, None]
    col_ids = order[:, my_col, :] * grid_size + residues[:, None]
    row_blocks = which_map[row_ids]
    halves_of = row_blocks[:, 0] % group_count // grid_size

    def pick(target_half):
        hit = halves_of == target_half
        chosen = jnp.argsort(jnp.where(hit, 0, grid_size) + residues)[:cap]
        return chosen, hit[chosen]

    mine, valid = pick(my_half)
    other, _ = pick(1 - my_half)
    swapped = jnp.logical_not(
        use_direct(mine[:, None], residues[None, :], my_row, my_col)
    )
    lanes = jnp.arange(BE)
    row_perm = (which_inner[row_ids[mine]][:, :, None, :] == lanes[:, None]).astype(BF16)
    col_perm = (which_inner[col_ids][:, :, :, None] == lanes).astype(BF16)
    u_at = (which_map[col_ids] // grid_size).reshape(-1)
    return {
        "order": order,
        "mine": mine,
        "other": other,
        "valid": valid,
        "swapped": swapped.astype(jnp.int32).reshape(-1),
        "t_at": (row_blocks[mine] // group_count).reshape(-1),
        "u_at": u_at,
        "row_perm": row_perm,
        "col_perm": col_perm,
    }


def panel_column(received, rows, u_at, my_row, my_col, slots):
    side = slots * BE
    hit = u_at == 0
    found = jnp.any(hit)
    at = jnp.argmax(hit)
    s = at // slots
    k = at % slots
    pieces = []
    for a in range(rows.shape[0]):
        r = rows[a]
        straight = lax.dynamic_slice(received, (r, s, 0, k * BE), (1, 1, side, BE))[0, 0]
        across = lax.dynamic_slice(received, (r, s, k * BE, 0), (1, 1, BE, side))[0, 0]
        pieces.append(jnp.where(use_direct(r, s, my_row, my_col), straight, across.T))
    return jnp.where(found, jnp.stack(pieces), 0.0)


def panel_add(front_panel, columns, tables, slots):
    row_blocks = front_panel.shape[0]
    cap = columns.shape[0]
    at = jnp.argmax(tables["u_at"] == 0)
    col_perm = tables["col_perm"].reshape(-1, BE, BE)[at].astype(F32)
    blocks = columns.reshape(cap, slots, BE, BE)
    moved = jnp.einsum(
        "aixy,aiyz->aixz", tables["row_perm"].astype(F32), blocks, precision=HIGHEST
    )
    moved = jnp.dot(moved.reshape(-1, BE), col_perm, precision=HIGHEST).reshape(-1, BE, BE)
    t_of = jnp.where(jnp.repeat(tables["valid"], slots), tables["t_at"], -1)
    match = t_of[None, :] == jnp.arange(row_blocks)[:, None]
    picked = jnp.take(moved, jnp.argmax(match, axis=1), axis=0)
    return front_panel + jnp.where(jnp.any(match, axis=1)[:, None, None], picked, 0.0)


def on_device(front_init, child_update, child_map):
    grid_size = lax.axis_size("row")
    halves = lax.axis_size("half")
    group_count = halves * grid_size
    my_half = lax.axis_index("half")
    my_row = lax.axis_index("row")
    my_col = lax.axis_index("col")
    my_group = my_half * grid_size + my_row
    slots = child_update.shape[1] // BE // grid_size
    front_rows, front_cols = front_init.shape
    row_blocks = front_rows // BE
    cap = min(grid_size, row_blocks // slots)
    block_map = child_map.reshape(2, -1, BE)[:, :, 0] // BE
    inner_perm = child_map.reshape(2, -1, BE) % BE

    def tables(which):
        return child_tables(
            block_map[which], inner_perm[which], grid_size, group_count,
            my_row, my_col, my_half, cap, slots,
        )

    own = tables(my_half)
    far = tables(1 - my_half)

    packed = pack(
        child_update[0],
        own["order"][my_row].reshape(-1),
        own["order"][my_col].reshape(-1),
        grid_size,
        slots,
    )
    received = exchange(packed, grid_size)
    side = slots * BE

    swap_half = [(0, 1), (1, 0)]
    out_panel = panel_column(received, own["other"], own["u_at"], my_row, my_col, slots)
    far_panel = lax.ppermute(out_panel, "half", swap_half)
    outgoing = jnp.concatenate(
        [lax.dynamic_index_in_dim(received, own["other"][a], 0) for a in range(cap)], axis=0
    )
    outgoing, far_panel = lax.optimization_barrier((outgoing, far_panel))
    incoming = lax.ppermute(outgoing, "half", swap_half)

    own_panel = panel_column(received, own["mine"], own["u_at"], my_row, my_col, slots)
    panel = front_init[:, :BE].reshape(row_blocks, BE, BE)
    panel = panel_add(panel, own_panel, own, slots)
    panel = panel_add(panel, far_panel, far, slots)
    panel = panel.reshape(front_rows, BE)

    slab = lax.all_gather(panel, "col", axis=1, tiled=True)[:, :WIDE]
    diagonal = lax.all_gather(slab[:BE], ("half", "row"), axis=0, tiled=True)[:WIDE]
    pieces = []
    for k in range(grid_size):
        perm = [
            (a * grid_size + q, (q + k) % grid_size * grid_size + a)
            for a in range(grid_size)
            for q in range(grid_size)
        ]
        pieces.append(lax.ppermute(panel, ("row", "col"), perm))
    pieces = jnp.stack(pieces)
    pieces = jnp.take(pieces, (my_row - jnp.arange(WIDE // BE)) % grid_size, axis=0)
    near_rows = pieces.transpose(1, 0, 2).reshape(row_blocks, BE, WIDE)
    far_rows = lax.ppermute(near_rows, "half", swap_half)
    even = jnp.where(my_half == 0, near_rows, far_rows)
    odd = jnp.where(my_half == 0, far_rows, near_rows)
    column_side = jnp.stack([even, odd], axis=1).reshape(front_cols, WIDE)

    identity = jnp.eye(PANEL, dtype=F32)

    def inverse_of(block):
        factor = jnp.linalg.cholesky(block)
        return lax.linalg.triangular_solve(factor, identity, left_side=True, lower=True)

    inverse1 = inverse_of(diagonal[:PANEL, :PANEL])
    below = jnp.dot(diagonal[PANEL:, :PANEL], inverse1.T, precision=HIGHEST)
    inverse2 = inverse_of(
        diagonal[PANEL:, PANEL:] - jnp.dot(below, below.T, precision=HIGHEST)
    )

    def lower(rows, natural):
        first = jnp.dot(rows[:, :PANEL], inverse1.T, precision=HIGHEST)
        rest = rows[:, PANEL:] - jnp.dot(first, below.T, precision=HIGHEST)
        second = jnp.dot(rest, inverse2.T, precision=HIGHEST)
        second = jnp.where((natural >= PANEL)[:, None], second, 0.0)
        return jnp.concatenate([first, second], axis=1)

    row_ids = jnp.arange(front_rows)
    natural_rows = (row_ids // BE * group_count + my_group) * BE + row_ids % BE
    col_ids = jnp.arange(front_cols)
    natural_cols = (col_ids // BE * grid_size + my_col) * BE + col_ids % BE
    lrow = lower(slab, natural_rows)
    lcol = lower(column_side, natural_cols)

    residues = jnp.arange(grid_size)
    front = place(
        front_init,
        received.reshape(-1, side, side),
        (own["mine"][:, None] * grid_size + residues).reshape(-1),
        own["t_at"], own["u_at"], own["swapped"], own["valid"].astype(jnp.int32),
        own["row_perm"], own["col_perm"], grid_size,
    )
    front = place(
        front,
        incoming.reshape(-1, side, side),
        jnp.arange(cap * grid_size),
        far["t_at"], far["u_at"], far["swapped"], far["valid"].astype(jnp.int32),
        far["row_perm"], far["col_perm"], grid_size,
    )
    place_of = jnp.stack([my_group, my_col]).astype(jnp.int32)
    return update(front, lrow, lcol, place_of)


def solution(mesh):
    placed = (P(("half", "row"), "col"), P("half", "row", "col"), P())
    return jax.shard_map(
        on_device, mesh=mesh, in_specs=placed, out_specs=P(("half", "row"), "col"), check_vma=False
    )
```

time: 2040 us -> 858 us (0.42)
  waiting for transfers between devices: 1360 us -> 112 us
  Pallas kernels: 0 us -> 366 us
  local copies, waits for them, and re-layouts: 348 us -> 62.3 us
  other arithmetic: 242 us -> 137 us
  starting transfers between devices: 15.9 us -> 99.6 us
  between operations: 17.1 us -> 42.7 us
  matrix products: 51.8 us -> 30.1 us
    all_to_all x2 -> x0, waiting for transfers between devices: 885 us -> none  [the longest x1 705 us: on_device(): lax.all_to_all(packed, ('half', 'row'), split_axis=0, concat_axis=0, tile...]
    pallas_call x0 -> x5, Pallas kernels: none -> 366 us  [the longest x1 273 us: exchange(): pl.pallas_call(functools.partial(exchange_kernel, grid_size), out_shape=j...]
    all_gather x4 -> x2, waiting for transfers between devices: 327 us -> 0.01 us  [the longest x1 0.01 us: on_device(): slab = lax.all_gather(panel, 'col', axis=1, tiled=True)[:, :WIDE]]
    psum x2 -> x0, waiting for transfers between devices: 144 us -> none  [on_device(): diagonal = lax.psum(jnp.concatenate(pieces, axis=0), ('half', 'row'))]
    ppermute x0 -> x7, waiting for transfers between devices: none -> 112 us  [the longest x4 52.8 us: on_device(): pieces.append(lax.ppermute(panel, ('row', 'col'), perm))]
    ppermute x0 -> x7, starting transfers between devices: none -> 99.6 us  [the longest x4 96 us: on_device(): pieces.append(lax.ppermute(panel, ('row', 'col'), perm))]
    scatter-add x2 -> x0, other arithmetic: 85.1 us -> none  [on_device(): front_local = front_local.at[row_index].add(spread, mode='drop')]
    scatter x4 -> x0, local copies, waits for them, and re-layouts: 83.5 us -> none  [on_device(): spread = jnp.zeros((arrived.shape[1], front_cols), jnp.float32).at[:, col...]
  transfers between devices with their start and end apart: 8 -> 9, of which waited for: 8 -> 4; matrix products, arithmetic and copies ran while one was open for 2% -> 24% of each run, Pallas kernels for 0% -> 2%
where the time goes in v1:
time: 858 us; the launch traced here: 850 us
  Pallas kernels  366 us (43%)
  other arithmetic  137 us (16%)
  waiting for transfers between devices  112 us (13%)
  starting transfers between devices  99.6 us (12%)
  local copies, waits for them, and re-layouts  62.3 us (7%)
  between operations  42.7 us (5%)
  matrix products  30.1 us (4%)
    pallas_call x1, Pallas kernels, exchange(): pl.pallas_call(functools.partial(exchange_kernel, grid_size), out_shape=j...  273 us
    ppermute x4, starting transfers between devices, on_device(): pieces.append(lax.ppermute(panel, ('row', 'col'), perm))  96 us
    another operation x14, other arithmetic, inverse_of(): factor = jnp.linalg.cholesky(block)  69.4 us
    ppermute x4, waiting for transfers between devices, on_device(): pieces.append(lax.ppermute(panel, ('row', 'col'), perm))  52.8 us
    ppermute x1, waiting for transfers between devices, on_device(): far_rows = lax.ppermute(near_rows, 'half', swap_half)  44 us
    pallas_call x2, Pallas kernels, place(): pl.pallas_call(functools.partial(place_kernel, grid_size, slots, steps),...  41.8 us
    another operation x5, other arithmetic, inverse_of(): lax.linalg.triangular_solve(factor, identity, left_side=True, lower=True)  40.4 us
    pallas_call x1, Pallas kernels, update(): pl.pallas_call(update_kernel, grid_spec=pltpu.PrefetchScalarGridSpec(num_...  32.3 us
  transfers between devices with their start and end apart: 9, of which 4 were waited for; matrix products, arithmetic and copies ran while one was open for 24% of the time, Pallas kernels for 2%

profile of v1, /device:TPU:18, one launch (start us, length us, event | category | flops | bytes accessed | tf_op | source)
XLA Modules:
  0.0 849.6 jit_solution(13426540664274663720)
XLA Ops:
  37.2 18.6 %shard_map.37.src = f32[4,4,512,512]{3,2,1,0:T(8,128)} custom-call(s32[16]{0:T(128)} %reshape_squeeze.6.row_order, s32[16]{0:T(128)} %reshape_squeeze.7.col_order, f32[2048,2048]{1,0:T(8,128)} %bitcast.200), custom_call_target="tpu_custom_call" | custom-call | tf_op jit(solution)/shard_map/pallas_call | solution.py:38
  55.9 272.9 %shard_map.38 = f32[4,4,512,512]{3,2,1,0:T(8,128)} custom-call(f32[4,4,512,512]{3,2,1,0:T(8,128)} %shard_map.37.src), custom_call_target="tpu_custom_call" | custom-call | tf_op jit(solution)/shard_map/pallas_call | solution.py:161
  337.6 7.8 constant_dynamic-slice_fusion.5
  362.8 7.7 pad_maximum_fusion
  373.5 92.3 %collective-permute-start.5 = (f32[1280,128]{1,0:T(8,128)S(1)}, f32[1280,128]{1,0:T(8,128)S(1)}, u32[]{:S(2)}, u32[]{:S(2)}) collective-permute-start(f32[1280,128]{1,0:T(8,128)S(1)} %bitcast.203), channel_id=1, source_target_pairs={{0,12},{1,0},{2,4},{3,8},{4,13},{5,1},{6,5},{7,9},{8,14},{9,2},{10... | collective-permute-start | bytes 1966088 | tf_op jit(solution)/shard_map/ppermute | solution.py:443
  465.8 2.7 collective-permute-start.4
  469.5 36.3 %collective-permute-done.5 = f32[1280,128]{1,0:T(8,128)S(1)} collective-permute-done((f32[1280,128]{1,0:T(8,128)S(1)}, f32[1280,128]{1,0:T(8,128)S(1)}, u32[]{:S(2)}, u32[]{:S(2)}) %collective-permute-start.5) | collective-permute-done | bytes 655392 | tf_op jit(solution)/shard_map/ppermute | solution.py:443
  505.8 16.5 %collective-permute-done.4 = f32[1280,128]{1,0:T(8,128)S(1)} collective-permute-done((f32[1280,128]{1,0:T(8,128)S(1)}, f32[1280,128]{1,0:T(8,128)S(1)}, u32[]{:S(2)}, u32[]{:S(2)}) %collective-permute-start.4) | collective-permute-done | bytes 655392 | tf_op jit(solution)/shard_map/ppermute | solution.py:443
  528.4 5.4 copy.79
  538.5 18.8 %shard_map.39.front = f32[1280,2560]{1,0:T(8,128)S(1)} custom-call(s32[8]{0:T(128)S(1)} %add.601.chunk_at, s32[8]{0:T(128)S(1)} %get-tuple-element.65.t_at, s32[16]{0:T(128)S(1)} %and_select_fusion.3.u_at, s32[8]{0:T(128)S(1)} %reshape.632.swapped, s32[2]{0:T(128)S(1)} %convert_element_type.46.valid, f32[1280,2560]{1,0:T(8,128)} %front.1, ...), custom_call_target="tpu_custom_call" | custom-call | flops 4000000000 | bytes 36000000 | tf_op jit(solution)/shard_map/pallas_call | solution.py:228
  557.3 4.9 copy-done
  563.8 44.0 %collective-permute-done.6 = f32[10,128,512]{2,1,0:T(8,128)S(1)} collective-permute-done((f32[10,128,512]{2,1,0:T(8,128)}, f32[10,128,512]{2,1,0:T(8,128)S(1)}, u32[]{:S(2)}, u32[]{:S(2)}) %collective-permute-start.6) | collective-permute-done | bytes 2621472 | tf_op jit(solution)/shard_map/ppermute | solution.py:447
  609.3 2.9 copy.80
  614.4 11.7 %cholesky.130 = f32[128,128]{1,0:T(8,128)S(1)} custom-call(f32[128,128]{1,0:T(8,128)S(1)} %cholesky.194), custom_call_target="Cholesky" | custom-call | tf_op jit(solution)/shard_map/jit(cholesky)/cholesky | solution.py:455
  626.2 9.8 %custom-call.13 = f32[1,128,128]{1,2,0:T(8,128)S(1)} custom-call(f32[1,128,128]{2,1,0:T(8,128)S(1)} %get-tuple-element.97), custom_call_target="InvertDiagBlocksLowerTriangular" | custom-call | tf_op jit(solution)/shard_map/jit(cholesky)/cholesky | solution.py:455
  636.5 11.8 %cholesky.147 = f32[128,128]{1,0:T(8,128)S(1)} custom-call(f32[128,128]{1,0:T(8,128)S(1)} %convolution_subtract_fusion.6), custom_call_target="Cholesky" | custom-call | tf_op jit(solution)/shard_map/jit(cholesky)/cholesky | solution.py:455
  651.2 4.2 while.4
  655.4 19.7 %custom-call.14 = f32[2,128,128]{1,2,0:T(8,128)S(1)} custom-call(f32[2,128,128]{2,1,0:T(8,128)S(1)} %get-tuple-element.44), custom_call_target="InvertDiagBlocksLowerTriangular" | custom-call | tf_op jit(solution)/shard_map/triangular_solve/custom-call.0 | solution.py:456
  679.9 11.7 %cholesky.164 = f32[128,128]{1,0:T(8,128)S(1)} custom-call(f32[128,128]{1,0:T(8,128)S(1)} %cholesky.197), custom_call_target="Cholesky" | custom-call | tf_op jit(solution)/shard_map/jit(cholesky)/cholesky | solution.py:455
  691.6 9.8 %custom-call.15 = f32[1,128,128]{1,2,0:T(8,128)S(1)} custom-call(f32[1,128,128]{2,1,0:T(8,128)S(1)} %get-tuple-element.93), custom_call_target="InvertDiagBlocksLowerTriangular" | custom-call | tf_op jit(solution)/shard_map/jit(cholesky)/cholesky | solution.py:455
  701.9 11.7 %cholesky.181 = f32[128,128]{1,0:T(8,128)S(1)} custom-call(f32[128,128]{1,0:T(8,128)S(1)} %convolution_subtract_fusion.5), custom_call_target="Cholesky" | custom-call | tf_op jit(solution)/shard_map/jit(cholesky)/cholesky | solution.py:455
  716.2 3.8 while.5
  720.7 20.7 %custom-call.16 = f32[2,128,128]{1,2,0:T(8,128)} custom-call(f32[2,128,128]{2,1,0:T(8,128)S(1)} %get-tuple-element.45), custom_call_target="InvertDiagBlocksLowerTriangular" | custom-call | tf_op jit(solution)/shard_map/triangular_solve/custom-call.0 | solution.py:456
  741.4 2.6 fusion.2
  745.6 4.3 fusion
  755.7 3.3 convolution_subtract_fusion.1
  759.0 2.3 convolution_select_fusion.1
  762.2 4.5 convolution_subtract_fusion
  769.1 3.2 pad_maximum_fusion.2.lcol
  772.3 15.1 %collective-permute-done.1 = f32[2,4,512,512]{3,2,1,0:T(8,128)} collective-permute-done((f32[2,4,512,512]{3,2,1,0:T(8,128)}, f32[2,4,512,512]{3,2,1,0:T(8,128)}, u32[]{:S(2)}, u32[]{:S(2)}) %collective-permute-start.1) | collective-permute-done | bytes 8388640 | tf_op jit(solution)/shard_map/ppermute | solution.py:426
  787.4 22.9 %shard_map.40.front = f32[1280,2560]{1,0:T(8,128)} custom-call(s32[8]{0:T(128)S(1)} %iota.187.chunk_at, s32[8]{0:T(128)S(1)} %get-tuple-element.67.t_at, s32[16]{0:T(128)S(1)} %and_select_fusion.9.u_at, s32[8]{0:T(128)S(1)} %reshape.631.swapped, s32[2]{0:T(128)S(1)} %convert_element_type.43.valid, f32[1280,2560]{1,0:T(8,128)} %copy-done, ...), custom_call_target="tpu_custom_call" | custom-call | flops 4000000000 | bytes 36000000 | tf_op jit(solution)/shard_map/pallas_call | solution.py:228
  810.3 32.3 %shard_map.41 = f32[1280,2560]{1,0:T(8,128)} custom-call(s32[2]{0:T(128)S(1)} %pad_add_fusion.place_of, f32[1280,2560]{1,0:T(8,128)} %shard_map.40.front, f32[1280,512]{1,0:T(8,128)S(1)} %pad_maximum_fusion.3.lrow, f32[2560,512]{1,0:T(8,128)} %pad_maximum_fusion.2.lcol), custom_call_target="tpu_custom_call" | custom-call | flops 10000000000 | bytes 34000000 | tf_op jit(solution)/shard_map/pallas_call | solution.py:292
  (246 shorter events, 78.4 us)
Async XLA Ops:
  6.5 518.2 %all-gather.3.cloned.1.call-start = ((), (), s32[]{:S(2)}) async-start(), calls=%async_computation | async-start | bytes 3276800 | tf_op jit(solution)/shard_map/all_gather | solution.py:434
  332.8 4.7 copy-start.11
  335.9 34.6 %collective-permute-start = (f32[2,512,128]{2,1,0:T(8,128)S(1)}, f32[2,512,128]{2,1,0:T(8,128)S(1)}, u32[]{:S(2)}, u32[]{:S(2)}) collective-permute-start(f32[2,512,128]{2,1,0:T(8,128)S(1)} %maximum_select_fusion), channel_id=1, source_target_pairs={{0,16},{16,0},{1,17},{17,1},{2,18},{18,2},{3,19},{19,3},{4,20},{20... | collective-permute-start | bytes 1572872 | tf_op jit(solution)/shard_map/ppermute | solution.py:421
  370.5 1.5 slice-start.2
  373.5 238.8 %all-gather.5.cloned.1.call-start = ((), (), s32[]{:S(2)}) async-start(), calls=%async_computation.1 | async-start | bytes 2359296 | tf_op jit(solution)/shard_map/all_gather | solution.py:435
  373.5 132.3 %collective-permute-start.5 = (f32[1280,128]{1,0:T(8,128)S(1)}, f32[1280,128]{1,0:T(8,128)S(1)}, u32[]{:S(2)}, u32[]{:S(2)}) collective-permute-start(f32[1280,128]{1,0:T(8,128)S(1)} %bitcast.203), channel_id=1, source_target_pairs={{0,12},{1,0},{2,4},{3,8},{4,13},{5,1},{6,5},{7,9},{8,14},{9,2},{10... | collective-permute-start | bytes 1966088 | tf_op jit(solution)/shard_map/ppermute | solution.py:443
  465.8 56.5 %collective-permute-start.4 = (f32[1280,128]{1,0:T(8,128)S(1)}, f32[1280,128]{1,0:T(8,128)S(1)}, u32[]{:S(2)}, u32[]{:S(2)}) collective-permute-start(f32[1280,128]{1,0:T(8,128)S(1)} %bitcast.204), channel_id=1, source_target_pairs={{0,8},{1,12},{2,0},{3,4},{4,9},{5,13},{6,1},{7,5},{8,10},{9,14},{1... | collective-permute-start | bytes 1966088 | tf_op jit(solution)/shard_map/ppermute | solution.py:443
  468.5 53.8 %collective-permute-start.3 = (f32[1280,128]{1,0:T(8,128)S(1)}, f32[1280,128]{1,0:T(8,128)S(1)}, u32[]{:S(2)}, u32[]{:S(2)}) collective-permute-start(f32[1280,128]{1,0:T(8,128)S(1)} %bitcast.205), channel_id=1, source_target_pairs={{0,4},{1,8},{2,12},{3,0},{4,5},{5,9},{6,13},{7,1},{8,6},{9,10},{10... | collective-permute-start | bytes 1966088 | tf_op jit(solution)/shard_map/ppermute | solution.py:443
  468.5 53.8 %collective-permute-start.2 = (f32[1280,128]{1,0:T(8,128)S(1)}, f32[1280,128]{1,0:T(8,128)S(1)}, u32[]{:S(2)}, u32[]{:S(2)}) collective-permute-start(f32[1280,128]{1,0:T(8,128)S(1)} %bitcast.206), channel_id=1, source_target_pairs={{0,0},{1,4},{2,8},{3,12},{4,1},{5,5},{6,9},{7,13},{8,2},{9,6},{10,... | collective-permute-start | bytes 1966088 | tf_op jit(solution)/shard_map/ppermute | solution.py:443
  536.0 71.9 %collective-permute-start.6 = (f32[10,128,512]{2,1,0:T(8,128)}, f32[10,128,512]{2,1,0:T(8,128)S(1)}, u32[]{:S(2)}, u32[]{:S(2)}) collective-permute-start(f32[10,128,512]{2,1,0:T(8,128)} %reshape.605), channel_id=1, source_target_pairs={{0,16},{16,0},{1,17},{17,1},{2,18},{18,2},{3,19},{19,3},{4,20},{20... | collective-permute-start | bytes 7864328 | tf_op jit(solution)/shard_map/ppermute | solution.py:447
  538.5 69.4 %copy-start.3 = (f32[10,128,512]{2,1,0:T(8,128)S(1)}, f32[10,128,512]{2,1,0:T(8,128)}, u32[]{:S(2)}) copy-start(f32[10,128,512]{2,1,0:T(8,128)} %reshape.605) | copy-start | bytes 7864324
  557.3 5.0 copy-start
  562.3 225.1 %collective-permute-start.1 = (f32[2,4,512,512]{3,2,1,0:T(8,128)}, f32[2,4,512,512]{3,2,1,0:T(8,128)}, u32[]{:S(2)}, u32[]{:S(2)}) collective-permute-start(f32[2,4,512,512]{3,2,1,0:T(8,128)} %pad_maximum_fusion), channel_id=1, source_target_pairs={{0,16},{16,0},{1,17},{17,1},{2,18},{18,2},{3,19},{19,3},{4,20},{20... | collective-permute-start | bytes 25165832 | tf_op jit(solution)/shard_map/ppermute | solution.py:426
  612.2 62.8 %copy-start.8 = (f32[256,256]{1,0:T(8,128)S(1)}, f32[256,256]{1,0:T(8,128)}, u32[]{:S(2)}) copy-start(f32[256,256]{1,0:T(8,128)} %fusion.23) | copy-start | bytes 786436
  675.4 66.0 %copy-start.7 = (f32[128,256]{1,0:T(8,128)}, f32[128,256]{1,0:T(8,128)S(1)}, u32[]{:S(2)}) copy-start(f32[128,256]{1,0:T(8,128)S(1)} %fusion.27) | copy-start | bytes 393220
  676.0 65.4 %copy-start.9 = (f32[128,256]{1,0:T(8,128)}, f32[128,256]{1,0:T(8,128)S(1)}, u32[]{:S(2)}) copy-start(f32[128,256]{1,0:T(8,128)S(1)} %fusion.35) | copy-start | bytes 393220
  677.6 0.7 copy-start.4
  720.0 0.7 copy-start.10
  744.1 1.6 copy-start.1
  755.7 5.6 copy-start.6
  755.7 6.0 slice-start
  759.0 2.8 slice-start.1
  761.3 1.0 copy-start.5
  766.8 2.3 copy-start.2
Sparse Core Ops, SparseCore 0:
  373.6 139.3 all-gather.2
  526.5 64.8 all-gather.4

commit v2 on v1

--- a/solution.py
+++ b/solution.py
@@ -49,7 +49,10 @@
     )(row_order, col_order, child)
 
 
-def exchange_kernel(grid_size, src, dst, send_direct, send_swap, recv, local):
+def exchange_kernel(
+    grid_size, src, dst, relay, send_direct, send_swap, recv, local,
+    relay_recv, relay_send,
+):
     r = lax.axis_index("row")
     s = lax.axis_index("col")
     half = lax.axis_index("half")
@@ -78,51 +81,132 @@
     def _():
         own_swap.start()
 
-    def direct_copy(k, x, y):
+    def turns(x, y):
+        return jnp.logical_and(x != r, y // 2 != s // 2)
+
+    def first_hop(kind, k, x, y):
+        source = src.at[y, x] if kind else src.at[x, y]
         return pltpu.make_async_remote_copy(
-            src_ref=src.at[x, y],
-            dst_ref=dst.at[r, s],
-            send_sem=send_direct.at[k],
-            recv_sem=recv.at[r * g + s],
+            src_ref=source,
+            dst_ref=relay.at[s, x, kind],
+            send_sem=(send_swap if kind else send_direct).at[k],
+            recv_sem=relay_recv.at[(s * g + x) * 2 + kind],
+            device_id=(half, r, y),
+            device_id_type=pl.DeviceIdType.MESH,
+        )
+
+    def second_hop(kind, b, x):
+        at = (b * g + x) * 2 + kind
+        target, slot = (dst.at[b, r], b * g + r) if kind else (dst.at[r, b], r * g + b)
+        return pltpu.make_async_remote_copy(
+            src_ref=relay.at[b, x, kind],
+            dst_ref=target,
+            send_sem=relay_send.at[at],
+            recv_sem=recv.at[slot],
+            device_id=(half, x, s),
+            device_id_type=pl.DeviceIdType.MESH,
+        )
+
+    def whole_way(kind, k, x, y):
+        source, target, slot = (
+            (src.at[y, x], dst.at[s, r], s * g + r)
+            if kind
+            else (src.at[x, y], dst.at[r, s], r * g + s)
+        )
+        return pltpu.make_async_remote_copy(
+            src_ref=source,
+            dst_ref=target,
+            send_sem=(send_swap if kind else send_direct).at[k],
+            recv_sem=recv.at[slot],
             device_id=(half, x, y),
             device_id_type=pl.DeviceIdType.MESH,
         )
 
-    def swap_copy(k, x, y):
-        return pltpu.make_async_remote_copy(
-            src_ref=src.at[y, x],
-            dst_ref=dst.at[s, r],
-            send_sem=send_swap.at[k],
-            recv_sem=recv.at[s * g + r],
-            device_id=(half, x, y),
-            device_id_type=pl.DeviceIdType.MESH,
-        )
-
-    def send(k, carry):
+    def wanted(kind, a, b, x, y):
+        if kind:
+            return jnp.logical_not(use_direct(b, a, x, y))
+        return use_direct(a, b, x, y)
+
+    def send_turning(k, carry):
         x, y = peer(k)
-
-        @pl.when(use_direct(r, s, x, y))
-        def _():
-            direct_copy(k, x, y).start()
-
-        @pl.when(jnp.logical_not(use_direct(s, r, x, y)))
-        def _():
-            swap_copy(k, x, y).start()
-
-        return carry
-
-    lax.fori_loop(1, g * g, send, 0)
+        for kind in range(2):
+
+            @pl.when(jnp.logical_and(turns(x, y), wanted(kind, r, s, x, y)))
+            def _():
+                first_hop(kind, k, x, y).start()
+
+        return carry
+
+    lax.fori_loop(1, g * g, send_turning, 0)
+
+    def send_straight(k, carry):
+        x, y = peer(k)
+        for kind in range(2):
+
+            @pl.when(
+                jnp.logical_and(
+                    jnp.logical_not(turns(x, y)), wanted(kind, r, s, x, y)
+                )
+            )
+            def _():
+                whole_way(kind, k, x, y).start()
+
+        return carry
+
+    lax.fori_loop(1, g * g, send_straight, 0)
+
+    def relayed(k):
+        x = (r + k // g) % g
+        b = (s + g - k % g) % g
+        return b, x
+
+    def pass_on(k, carry):
+        b, x = relayed(k)
+        for kind in range(2):
+
+            @pl.when(
+                jnp.logical_and(
+                    jnp.logical_and(x != r, b // 2 != s // 2), wanted(kind, r, b, x, s)
+                )
+            )
+            def _():
+                pltpu.make_async_remote_copy(
+                    src_ref=src.at[x, b],
+                    dst_ref=relay.at[b, x, kind],
+                    send_sem=send_direct.at[0],
+                    recv_sem=relay_recv.at[(b * g + x) * 2 + kind],
+                    device_id=(half, r, (s + 1) % g),
+                    device_id_type=pl.DeviceIdType.MESH,
+                ).wait_recv()
+                second_hop(kind, b, x).start()
+
+        return carry
+
+    lax.fori_loop(1, g * g, pass_on, 0)
+
+    def passed_on(k, carry):
+        b, x = relayed(k)
+        for kind in range(2):
+
+            @pl.when(
+                jnp.logical_and(
+                    jnp.logical_and(x != r, b // 2 != s // 2), wanted(kind, r, b, x, s)
+                )
+            )
+            def _():
+                second_hop(kind, b, x).wait_send()
+
+        return carry
+
+    lax.fori_loop(1, g * g, passed_on, 0)
 
     def sent(k, carry):
         x, y = peer(k)
-
-        @pl.when(use_direct(r, s, x, y))
-        def _():
-            direct_copy(k, x, y).wait_send()
-
-        @pl.when(jnp.logical_not(use_direct(s, r, x, y)))
-        def _():
-            swap_copy(k, x, y).wait_send()
+        for kind in range(2):
+
+            @pl.when(wanted(kind, r, s, x, y))
+            def _():
+                whole_way(kind, k, x, y).wait_send()
 
         return carry
 
@@ -160,17 +244,22 @@
     n = grid_size * grid_size
     return pl.pallas_call(
         functools.partial(exchange_kernel, grid_size),
-        out_shape=jax.ShapeDtypeStruct(packed.shape, F32),
+        out_shape=[
+            jax.ShapeDtypeStruct(packed.shape, F32),
+            jax.ShapeDtypeStruct((grid_size, grid_size, 2) + packed.shape[2:], F32),
+        ],
         in_specs=[pl.BlockSpec(memory_space=pl.ANY)],
-        out_specs=pl.BlockSpec(memory_space=pl.ANY),
+        out_specs=[pl.BlockSpec(memory_space=pl.ANY)] * 2,
         scratch_shapes=[
             pltpu.SemaphoreType.DMA((n,)),
             pltpu.SemaphoreType.DMA((n,)),
             pltpu.SemaphoreType.DMA((n,)),
             pltpu.SemaphoreType.DMA((2,)),
+            pltpu.SemaphoreType.DMA((2 * n,)),
+            pltpu.SemaphoreType.DMA((2 * n,)),
         ],
         compiler_params=pltpu.CompilerParams(collective_id=0, has_side_effects=True),
-    )(packed)
+    )(packed)[0]
 
 
 def place_kernel(
@@ -449,24 +538,32 @@
     odd = jnp.where(my_half == 0, far_rows, near_rows)
     column_side = jnp.stack([even, odd], axis=1).reshape(front_cols, WIDE)
 
-    identity = jnp.eye(PANEL, dtype=F32)
-
-    def inverse_of(block):
-        factor = jnp.linalg.cholesky(block)
-        return lax.linalg.triangular_solve(factor, identity, left_side=True, lower=True)
-
-    inverse1 = inverse_of(diagonal[:PANEL, :PANEL])
-    below = jnp.dot(diagonal[PANEL:, :PANEL], inverse1.T, precision=HIGHEST)
-    inverse2 = inverse_of(
-        diagonal[PANEL:, PANEL:] - jnp.dot(below, below.T, precision=HIGHEST)
-    )
+    identity = jnp.eye(BE, dtype=F32)
+    block_of = jnp.arange(WIDE) // BE
+
+    def eliminate(k, carry):
+        schur, inverse = carry
+        at = k * BE
+        block = lax.dynamic_slice(schur, (at, at), (BE, BE))
+        factor = lax.linalg.cholesky(block, symmetrize_input=False)
+        small = lax.linalg.triangular_solve(factor, identity, left_side=True, lower=True)
+        below = jnp.dot(
+            lax.dynamic_slice(schur, (0, at), (WIDE, BE)), small.T, precision=HIGHEST
+        )
+        below = jnp.where((block_of > k)[:, None], below, 0.0)
+        schur = schur - jnp.dot(below, below.T, precision=HIGHEST)
+        mine = jnp.dot(
+            small, lax.dynamic_slice(inverse, (at, 0), (BE, WIDE)), precision=HIGHEST
+        )
+        inverse = inverse - jnp.dot(below, mine, precision=HIGHEST)
+        return schur, lax.dynamic_update_slice(inverse, mine, (at, 0))
+
+    _, inverse = lax.fori_loop(0, WIDE // BE, eliminate, (diagonal, jnp.eye(WIDE, dtype=F32)))
 
     def lower(rows, natural):
-        first = jnp.dot(rows[:, :PANEL], inverse1.T, precision=HIGHEST)
-        rest = rows[:, PANEL:] - jnp.dot(first, below.T, precision=HIGHEST)
-        second = jnp.dot(rest, inverse2.T, precision=HIGHEST)
-        second = jnp.where((natural >= PANEL)[:, None], second, 0.0)
-        return jnp.concatenate([first, second], axis=1)
+        full = jnp.dot(rows, inverse.T, precision=HIGHEST)
+        second = (jnp.arange(WIDE) >= PANEL)[None, :] & (natural < PANEL)[:, None]
+        return jnp.where(second, 0.0, full)
 
     row_ids = jnp.arange(front_rows)
     natural_rows = (row_ids // BE * group_count + my_group) * BE + row_ids % BE

time: 858 us -> 727 us (0.85)
  Pallas kernels: 366 us -> 276 us
  starting transfers between devices: 99.6 us -> 56.5 us
  waiting for transfers between devices: 112 us -> 143 us
  other arithmetic: 137 us -> 117 us
  local copies, waits for them, and re-layouts: 62.3 us -> 47.9 us
    pallas_call x1, Pallas kernels: 273 us -> 184 us  [exchange(): pl.pallas_call(functools.partial(exchange_kernel, grid_size), out_shape=[...]
    ppermute x4, starting transfers between devices: 96 us -> 52.4 us  [on_device(): pieces.append(lax.ppermute(panel, ('row', 'col'), perm))]
    ppermute x1, waiting for transfers between devices: 15.1 us -> 46.1 us  [on_device(): incoming = lax.ppermute(outgoing, 'half', swap_half)]
    another operation x19 -> x20, other arithmetic: 110 us -> 91.2 us  [the longest x12 49.6 us: eliminate(): factor = lax.linalg.cholesky(block, symmetrize_input=False)]
    dot_general x8 -> x18, matrix products: 22.2 us -> 29.7 us  [the longest x2 16.9 us: lower(): full = jnp.dot(rows, inverse.T, precision=HIGHEST)]
  transfers between devices with their start and end apart: 9 -> 9, of which waited for: 4 -> 5; matrix products, arithmetic and copies ran while one was open for 24% -> 24% of each run, Pallas kernels for 2% -> 3%
where the time goes in v2:
time: 727 us; the launch traced here: 715 us
  Pallas kernels  276 us (38%)
  waiting for transfers between devices  143 us (20%)
  other arithmetic  117 us (16%)
  starting transfers between devices  56.5 us (8%)
  local copies, waits for them, and re-layouts  47.9 us (7%)
  between operations  41 us (6%)
  matrix products  33.1 us (5%)
    pallas_call x1, Pallas kernels, exchange(): pl.pallas_call(functools.partial(exchange_kernel, grid_size), out_shape=[...  184 us
    ppermute x4, starting transfers between devices, on_device(): pieces.append(lax.ppermute(panel, ('row', 'col'), perm))  52.4 us
    ppermute x4, waiting for transfers between devices, on_device(): pieces.append(lax.ppermute(panel, ('row', 'col'), perm))  50.8 us
    another operation x12, other arithmetic, eliminate(): factor = lax.linalg.cholesky(block, symmetrize_input=False)  49.6 us
    ppermute x1, waiting for transfers between devices, on_device(): far_rows = lax.ppermute(near_rows, 'half', swap_half)  46.5 us
    ppermute x1, waiting for transfers between devices, on_device(): incoming = lax.ppermute(outgoing, 'half', swap_half)  46.1 us
    another operation x8, other arithmetic, eliminate(): lax.linalg.triangular_solve(factor, identity, left_side=True, lower=True)  41.6 us
    pallas_call x2, Pallas kernels, place(): pl.pallas_call(functools.partial(place_kernel, grid_size, slots, steps),...  40.6 us
  transfers between devices with their start and end apart: 9, of which 5 were waited for; matrix products, arithmetic and copies ran while one was open for 24% of the time, Pallas kernels for 3%

profile of v2, /device:TPU:18, one launch (start us, length us, event | category | flops | bytes accessed | tf_op | source)
XLA Modules:
  0.0 715.3 jit_solution(17917616378868037636)
XLA Ops:
  40.5 18.7 %shard_map.37.src = f32[4,4,512,512]{3,2,1,0:T(8,128)} custom-call(s32[16]{0:T(128)} %reshape_squeeze.6.row_order, s32[16]{0:T(128)} %reshape_squeeze.7.col_order, f32[2048,2048]{1,0:T(8,128)} %bitcast.158), custom_call_target="tpu_custom_call" | custom-call | tf_op jit(solution)/shard_map/pallas_call | solution.py:38
  59.2 184.0 %shard_map.38 = (f32[4,4,512,512]{3,2,1,0:T(8,128)}, f32[4,4,2,512,512]{4,3,2,1,0:T(8,128)}) custom-call(f32[4,4,512,512]{3,2,1,0:T(8,128)} %shard_map.37.src), custom_call_target="tpu_custom_call" | custom-call | tf_op jit(solution)/shard_map/pallas_call | solution.py:245
  250.0 7.8 %constant_dynamic-slice_fusion.3 = (f32[1,4,512,512]{3,2,1,0:T(8,128)}, f32[1,4,512,512]{3,2,1,0:T(8,128)}) fusion(f32[4,4,512,512]{3,2,1,0:T(8,128)} %get-tuple-element.116, s32[]{:T(128)S(6)} %select_n.537, s32[]{:T(128)S(6)} %select_n.538), kind=kLoop, calls=%fused_computation.158 | loop fusion | bytes 16777224 | tf_op jit(solution)/shard_map/jit(dynamic_index_in_dim)/dynamic_slice | solution.py:512
  275.6 7.7 %pad_maximum_fusion = f32[2,4,512,512]{3,2,1,0:T(8,128)} fusion(f32[1,4,512,512]{3,2,1,0:T(8,128)} %get-tuple-element.161, f32[1,4,512,512]{3,2,1,0:T(8,128)} %get-tuple-element.160), kind=kLoop, calls=%fused_computation.47 | loop fusion | flops 2097152 | bytes 16777216 | tf_op jit(solution)/shard_map/concatenate | solution.py:511
  287.8 46.2 %collective-permute-start.3 = (f32[1280,128]{1,0:T(8,128)}, f32[1280,128]{1,0:T(8,128)S(1)}, u32[]{:S(2)}, u32[]{:S(2)}) collective-permute-start(f32[1280,128]{1,0:T(8,128)} %bitcast.162), channel_id=1, source_target_pairs={{0,4},{1,8},{2,12},{3,0},{4,5},{5,9},{6,13},{7,1},{8,6},{9,10},{10... | collective-permute-start | bytes 1966088 | tf_op jit(solution)/shard_map/ppermute | solution.py:532
  334.0 4.5 collective-permute-start.5
  338.5 29.6 %collective-permute-done.3 = f32[1280,128]{1,0:T(8,128)S(1)} collective-permute-done((f32[1280,128]{1,0:T(8,128)}, f32[1280,128]{1,0:T(8,128)S(1)}, u32[]{:S(2)}, u32[]{:S(2)}) %collective-permute-start.3) | collective-permute-done | bytes 655392 | tf_op jit(solution)/shard_map/ppermute | solution.py:532
  368.1 9.9 %collective-permute-done.4 = f32[1280,128]{1,0:T(8,128)S(1)} collective-permute-done((f32[1280,128]{1,0:T(8,128)}, f32[1280,128]{1,0:T(8,128)S(1)}, u32[]{:S(2)}, u32[]{:S(2)}) %collective-permute-start.4) | collective-permute-done | bytes 655392 | tf_op jit(solution)/shard_map/ppermute | solution.py:532
  378.0 11.3 %collective-permute-done.5 = f32[1280,128]{1,0:T(8,128)S(1)} collective-permute-done((f32[1280,128]{1,0:T(8,128)}, f32[1280,128]{1,0:T(8,128)S(1)}, u32[]{:S(2)}, u32[]{:S(2)}) %collective-permute-start.5) | collective-permute-done | bytes 655392 | tf_op jit(solution)/shard_map/ppermute | solution.py:532
  389.5 2.2 gather_fusion.16
  395.4 5.4 copy.47
  400.8 2.2 reshape.619
  405.0 18.6 %shard_map.39.front = f32[1280,2560]{1,0:T(8,128)S(1)} custom-call(s32[8]{0:T(128)S(1)} %add.620.chunk_at, s32[8]{0:T(128)S(1)} %get-tuple-element.143.t_at, s32[16]{0:T(128)S(1)} %and_select_fusion.4.u_at, s32[8]{0:T(128)S(1)} %reshape.622.swapped, s32[2]{0:T(128)S(1)} %convert_element_type.47.valid, f32[1280,2560]{1,0:T(8,128)} %front.1, ...), custom_call_target="tpu_custom_call" | custom-call | flops 4000000000 | bytes 36000000 | tf_op jit(solution)/shard_map/pallas_call | solution.py:317
  423.7 4.9 copy-done
  428.6 2.0 collective-permute-start.1
  430.6 46.5 %collective-permute-done.6 = f32[10,128,512]{2,1,0:T(8,128)} collective-permute-done((f32[10,128,512]{2,1,0:T(8,128)}, f32[10,128,512]{2,1,0:T(8,128)}, u32[]{:S(2)}, u32[]{:S(2)}) %collective-permute-start.6) | collective-permute-done | bytes 2621472 | tf_op jit(solution)/shard_map/ppermute | solution.py:536
  477.2 2.4 select_bitcast_fusion.1
  480.4 3.0 copy.48
  484.6 106.1 %while.16 = (s32[]{:T(128)}, f32[512,512]{1,0:T(8,128)S(1)}, f32[512,512]{1,0:T(8,128)S(1)}, s32[]{:T(128)}, s32[]{:T(128)}, /*index=5*/s32[]{:T(128)}, s32[]{:T(128)}) while((s32[]{:T(128)}, f32[512,512]{1,0:T(8,128)S(1)}, f32[512,512]{1,0:T(8,128)S(1)}, s32[]{:T(128)}, s32[]{:T(128)}, /*index=5*/s32[]{:T(128)}, ...), condition=%wide.region_15.17_spmd.clone, body=%wide.region_12.16_spmd.clone.sunk | while | flops 1032540800 | bytes 7145617 | solution.py:561
  484.9 11.7 %cholesky.73 = f32[128,128]{1,0:T(8,128)S(1)} custom-call(f32[128,128]{1,0:T(8,128)S(1)} %dynamic_slice.154), custom_call_target="Cholesky" | custom-call | tf_op jit(solution)/shard_map/while/body/eval_jaxpr/cholesky | solution.py:548
  497.9 9.8 %custom-call.53 = f32[1,128,128]{1,2,0:T(8,128)S(1)} custom-call(f32[1,128,128]{2,1,0:T(8,128)S(1)} %fusion.134), custom_call_target="InvertDiagBlocksLowerTriangular" | custom-call | tf_op jit(solution)/shard_map/while/body/eval_jaxpr/triangular_solve | solution.py:549
  511.3 11.7 %cholesky.73 = f32[128,128]{1,0:T(8,128)S(1)} custom-call(f32[128,128]{1,0:T(8,128)S(1)} %dynamic_slice.154), custom_call_target="Cholesky" | custom-call | tf_op jit(solution)/shard_map/while/body/eval_jaxpr/cholesky | solution.py:548
  524.3 9.8 %custom-call.53 = f32[1,128,128]{1,2,0:T(8,128)S(1)} custom-call(f32[1,128,128]{2,1,0:T(8,128)S(1)} %fusion.134), custom_call_target="InvertDiagBlocksLowerTriangular" | custom-call | tf_op jit(solution)/shard_map/while/body/eval_jaxpr/triangular_solve | solution.py:549
  537.7 11.7 %cholesky.73 = f32[128,128]{1,0:T(8,128)S(1)} custom-call(f32[128,128]{1,0:T(8,128)S(1)} %dynamic_slice.154), custom_call_target="Cholesky" | custom-call | tf_op jit(solution)/shard_map/while/body/eval_jaxpr/cholesky | solution.py:548
  550.7 9.8 %custom-call.53 = f32[1,128,128]{1,2,0:T(8,128)S(1)} custom-call(f32[1,128,128]{2,1,0:T(8,128)S(1)} %fusion.134), custom_call_target="InvertDiagBlocksLowerTriangular" | custom-call | tf_op jit(solution)/shard_map/while/body/eval_jaxpr/triangular_solve | solution.py:549
  564.1 11.7 %cholesky.73 = f32[128,128]{1,0:T(8,128)S(1)} custom-call(f32[128,128]{1,0:T(8,128)S(1)} %dynamic_slice.154), custom_call_target="Cholesky" | custom-call | tf_op jit(solution)/shard_map/while/body/eval_jaxpr/cholesky | solution.py:548
  577.1 9.8 %custom-call.53 = f32[1,128,128]{1,2,0:T(8,128)S(1)} custom-call(f32[1,128,128]{2,1,0:T(8,128)S(1)} %fusion.134), custom_call_target="InvertDiagBlocksLowerTriangular" | custom-call | tf_op jit(solution)/shard_map/while/body/eval_jaxpr/triangular_solve | solution.py:549
  590.8 6.2 convolution_select_fusion.1.lrow
  597.0 10.7 %and_select_fusion.lcol = f32[2560,512]{1,0:T(8,128)} fusion(f32[2560,512]{1,0:T(8,128)S(1)} %bitcast.157, f32[512,512]{1,0:T(8,128)S(1)} %get-tuple-element.124, pred[512]{0:T(512)(128)(4,1)S(1)} %iota_compare_fusion.14, pred[2560]{0:T(1024)(128)(4,1)S(1)} %fusion.57), kind=kOutput, calls=%fused_computation.49 | convolution fusion | flops 8055685120 | bytes 11537408 | tf_op jit(solution)/shard_map/dot_general | solution.py:564
  607.7 46.1 %collective-permute-done.1 = f32[2,4,512,512]{3,2,1,0:T(8,128)} collective-permute-done((f32[2,4,512,512]{3,2,1,0:T(8,128)}, f32[2,4,512,512]{3,2,1,0:T(8,128)}, u32[]{:S(2)}, u32[]{:S(2)}) %collective-permute-start.1) | collective-permute-done | bytes 8388640 | tf_op jit(solution)/shard_map/ppermute | solution.py:515
  653.8 22.0 %shard_map.40.front = f32[1280,2560]{1,0:T(8,128)} custom-call(s32[8]{0:T(128)S(1)} %iota.202.chunk_at, s32[8]{0:T(128)S(1)} %get-tuple-element.145.t_at, s32[16]{0:T(128)S(1)} %and_select_fusion.10.u_at, s32[8]{0:T(128)S(1)} %reshape.621.swapped, s32[2]{0:T(128)S(1)} %convert_element_type.44.valid, f32[1280,2560]{1,0:T(8,128)} %copy-done, ...), custom_call_target="tpu_custom_call" | custom-call | flops 4000000000 | bytes 36000000 | tf_op jit(solution)/shard_map/pallas_call | solution.py:317
  675.8 32.3 %shard_map.41 = f32[1280,2560]{1,0:T(8,128)} custom-call(s32[2]{0:T(128)S(1)} %pad_add_fusion.place_of, f32[1280,2560]{1,0:T(8,128)} %shard_map.40.front, f32[1280,512]{1,0:T(8,128)S(1)} %convolution_select_fusion.1.lrow, f32[2560,512]{1,0:T(8,128)} %and_select_fusion.lcol), custom_call_target="tpu_custom_call" | custom-call | flops 10000000000 | bytes 34000000 | tf_op jit(solution)/shard_map/pallas_call | solution.py:381
  (214 shorter events, 63.1 us)
Async XLA Ops:
  6.5 385.1 %all-gather.3.cloned.1.call-start = ((), (), s32[]{:S(2)}) async-start(), calls=%async_computation | async-start | bytes 3276800 | tf_op jit(solution)/shard_map/all_gather | solution.py:523
  244.8 5.2 copy-start.3
  248.5 34.8 %collective-permute-start = (f32[2,512,128]{2,1,0:T(8,128)}, f32[2,512,128]{2,1,0:T(8,128)S(1)}, u32[]{:S(2)}, u32[]{:S(2)}) collective-permute-start(f32[2,512,128]{2,1,0:T(8,128)} %maximum_select_fusion), channel_id=1, source_target_pairs={{0,16},{16,0},{1,17},{17,1},{2,18},{18,2},{3,19},{19,3},{4,20},{20... | collective-permute-start | bytes 1572872 | tf_op jit(solution)/shard_map/ppermute | solution.py:510
  283.3 1.5 slice-start
  286.0 197.4 %all-gather.5.cloned.1.call-start = ((), (), s32[]{:S(2)}) async-start(), calls=%async_computation.1 | async-start | bytes 2359296 | tf_op jit(solution)/shard_map/all_gather | solution.py:524
  286.0 52.5 %collective-permute-start.2 = (f32[1280,128]{1,0:T(8,128)}, f32[1280,128]{1,0:T(8,128)S(1)}, u32[]{:S(2)}, u32[]{:S(2)}) collective-permute-start(f32[1280,128]{1,0:T(8,128)} %bitcast.161), channel_id=1, source_target_pairs={{0,0},{1,4},{2,8},{3,12},{4,1},{5,5},{6,9},{7,13},{8,2},{9,6},{10,... | collective-permute-start | bytes 1966088 | tf_op jit(solution)/shard_map/ppermute | solution.py:532
  287.8 80.3 %collective-permute-start.3 = (f32[1280,128]{1,0:T(8,128)}, f32[1280,128]{1,0:T(8,128)S(1)}, u32[]{:S(2)}, u32[]{:S(2)}) collective-permute-start(f32[1280,128]{1,0:T(8,128)} %bitcast.162), channel_id=1, source_target_pairs={{0,4},{1,8},{2,12},{3,0},{4,5},{5,9},{6,13},{7,1},{8,6},{9,10},{10... | collective-permute-start | bytes 1966088 | tf_op jit(solution)/shard_map/ppermute | solution.py:532
  334.0 44.0 %collective-permute-start.4 = (f32[1280,128]{1,0:T(8,128)}, f32[1280,128]{1,0:T(8,128)S(1)}, u32[]{:S(2)}, u32[]{:S(2)}) collective-permute-start(f32[1280,128]{1,0:T(8,128)} %bitcast.163), channel_id=1, source_target_pairs={{0,8},{1,12},{2,0},{3,4},{4,9},{5,13},{6,1},{7,5},{8,10},{9,14},{1... | collective-permute-start | bytes 1966088 | tf_op jit(solution)/shard_map/ppermute | solution.py:532
  334.0 55.3 %collective-permute-start.5 = (f32[1280,128]{1,0:T(8,128)}, f32[1280,128]{1,0:T(8,128)S(1)}, u32[]{:S(2)}, u32[]{:S(2)}) collective-permute-start(f32[1280,128]{1,0:T(8,128)} %bitcast.164), channel_id=1, source_target_pairs={{0,12},{1,0},{2,4},{3,8},{4,13},{5,1},{6,5},{7,9},{8,14},{9,2},{10... | collective-permute-start | bytes 1966088 | tf_op jit(solution)/shard_map/ppermute | solution.py:532
  403.0 74.2 %collective-permute-start.6 = (f32[10,128,512]{2,1,0:T(8,128)}, f32[10,128,512]{2,1,0:T(8,128)}, u32[]{:S(2)}, u32[]{:S(2)}) collective-permute-start(f32[10,128,512]{2,1,0:T(8,128)} %reshape.619), channel_id=1, source_target_pairs={{0,16},{16,0},{1,17},{17,1},{2,18},{18,2},{3,19},{19,3},{4,20},{20... | collective-permute-start | bytes 7864328 | tf_op jit(solution)/shard_map/ppermute | solution.py:536
  405.0 72.1 %copy-start.2 = (f32[10,128,512]{2,1,0:T(8,128)S(1)}, f32[10,128,512]{2,1,0:T(8,128)}, u32[]{:S(2)}) copy-start(f32[10,128,512]{2,1,0:T(8,128)} %reshape.619) | copy-start | bytes 7864324
  423.7 5.0 copy-start
  428.6 225.2 %collective-permute-start.1 = (f32[2,4,512,512]{3,2,1,0:T(8,128)}, f32[2,4,512,512]{3,2,1,0:T(8,128)}, u32[]{:S(2)}, u32[]{:S(2)}) collective-permute-start(f32[2,4,512,512]{3,2,1,0:T(8,128)} %pad_maximum_fusion), channel_id=1, source_target_pairs={{0,16},{16,0},{1,17},{17,1},{2,18},{18,2},{3,19},{19,3},{4,20},{20... | collective-permute-start | bytes 25165832 | tf_op jit(solution)/shard_map/ppermute | solution.py:515
  590.7 6.2 copy-start.1
Sparse Core Ops, SparseCore 0:
  286.1 94.3 all-gather.2
  393.5 65.9 all-gather.4

commit v3 on v2

--- a/solution.py
+++ b/solution.py
@@ -264,8 +264,9 @@
 
 def place_kernel(
     grid_size, slots, steps, chunk_at, t_at, u_at, swapped, valid,
-    front, chunk, row_perm, col_perm, out, acc, work, mid, sem,
+    front, row_perm, col_perm, *rest,
 ):
+    *chunks, out, acc, work, mid, sem = rest
     n = pl.program_id(0)
     a = n // grid_size
     s = n % grid_size
@@ -278,13 +279,16 @@
 
     @pl.when(valid[a] == 1)
     def _():
-        @pl.when(swapped[n] == 1)
-        def _():
-            work[...] = chunk[0].T
-
-        @pl.when(swapped[n] == 0)
-        def _():
-            work[...] = chunk[0]
+        for q, chunk in enumerate(chunks):
+            here = a == q if len(chunks) > 1 else a >= 0
+
+            @pl.when(jnp.logical_and(here, swapped[n] == 1))
+            def _():
+                work[...] = chunk[0].T
+
+            @pl.when(jnp.logical_and(here, swapped[n] == 0))
+            def _():
+                work[...] = chunk[0]
 
         for i in range(slots):
             t = pl.multiple_of(t_at[a * slots + i] * BE, BE)
@@ -314,6 +318,15 @@
     slots = row_perm.shape[1]
     steps = row_perm.shape[0] * grid_size
     side = slots * BE
+
+    def chunk_spec(q):
+        if len(chunks) == 1:
+            return pl.BlockSpec((1, side, side), lambda n, ca, *_: (ca[n], 0, 0))
+        return pl.BlockSpec(
+            (1, side, side),
+            lambda n, *_: (jnp.clip(n - q * grid_size, 0, grid_size - 1), 0, 0),
+        )
+
     return pl.pallas_call(
         functools.partial(place_kernel, grid_size, slots, steps),
         grid_spec=pltpu.PrefetchScalarGridSpec(
@@ -321,10 +334,10 @@
             grid=(steps,),
             in_specs=[
                 pl.BlockSpec(memory_space=pl.ANY),
-                pl.BlockSpec((1, side, side), lambda n, ca, *_: (ca[n], 0, 0)),
                 pl.BlockSpec((1, slots, BE, BE), lambda n, *_: (n // grid_size, 0, 0, 0)),
                 pl.BlockSpec((1, slots, BE, BE), lambda n, *_: (n % grid_size, 0, 0, 0)),
-            ],
+            ]
+            + [chunk_spec(q) for q in range(len(chunks))],
             out_specs=pl.BlockSpec(memory_space=pl.ANY),
             scratch_shapes=[
                 pltpu.VMEM(front.shape, F32),
@@ -338,7 +351,7 @@
         cost_estimate=pl.CostEstimate(
             flops=4_000_000_000, bytes_accessed=36_000_000, transcendentals=0
         ),
-    )(chunk_at, t_at, u_at, swapped, valid, front, chunks, row_perm, col_perm)
+    )(chunk_at, t_at, u_at, swapped, valid, front, row_perm, col_perm, *chunks)
 
 
 def update_kernel(place_of, front, lrow, lcol, out, col_high, col_low):
@@ -508,11 +521,14 @@
     swap_half = [(0, 1), (1, 0)]
     out_panel = panel_column(received, own["other"], own["u_at"], my_row, my_col, slots)
     far_panel = lax.ppermute(out_panel, "half", swap_half)
-    outgoing = jnp.concatenate(
-        [lax.dynamic_index_in_dim(received, own["other"][a], 0) for a in range(cap)], axis=0
-    )
-    outgoing, far_panel = lax.optimization_barrier((outgoing, far_panel))
-    incoming = lax.ppermute(outgoing, "half", swap_half)
+    incoming = [
+        lax.ppermute(
+            lax.dynamic_index_in_dim(received, own["other"][a], 0, keepdims=False),
+            "half",
+            swap_half,
+        )
+        for a in range(cap)
+    ]
 
     own_panel = panel_column(received, own["mine"], own["u_at"], my_row, my_col, slots)
     panel = front_init[:, :BE].reshape(row_blocks, BE, BE)
@@ -575,14 +591,14 @@
     residues = jnp.arange(grid_size)
     front = place(
         front_init,
-        received.reshape(-1, side, side),
+        [received.reshape(-1, side, side)],
         (own["mine"][:, None] * grid_size + residues).reshape(-1),
         own["t_at"], own["u_at"], own["swapped"], own["valid"].astype(jnp.int32),
         own["row_perm"], own["col_perm"], grid_size,
     )
     front = place(
         front,
-        incoming.reshape(-1, side, side),
+        incoming,
         jnp.arange(cap * grid_size),
         far["t_at"], far["u_at"], far["swapped"], far["valid"].astype(jnp.int32),
         far["row_perm"], far["col_perm"], grid_size,

time: 727 us -> 786 us (1.081)
  waiting for transfers between devices: 143 us -> 211 us
  other arithmetic: 117 us -> 108 us
    ppermute x1, waiting for transfers between devices: 46.5 us -> 171 us  [on_device(): far_rows = lax.ppermute(near_rows, 'half', swap_half)]
    ppermute x1 -> x2, waiting for transfers between devices: 46.1 us -> 0.01 us  [on_device(): lax.ppermute(lax.dynamic_index_in_dim(received, own['other'][a], 0, keepd...]
    ppermute x4, waiting for transfers between devices: 50.8 us -> 40.5 us  [on_device(): pieces.append(lax.ppermute(panel, ('row', 'col'), perm))]
    squeeze x0 -> x1, local copies, waits for them, and re-layouts: none -> 8.21 us  [on_device(): lax.dynamic_index_in_dim(received, own['other'][a], 0, keepdims=False)]
  transfers between devices with their start and end apart: 9 -> 10, of which waited for: 5 -> 4; matrix products, arithmetic and copies ran while one was open for 24% -> 6% of each run, Pallas kernels for 3% -> 5%
where the time goes in v3:
time: 786 us; the launch traced here: 776 us
  Pallas kernels  277 us (35%)
  waiting for transfers between devices  211 us (27%)
  other arithmetic  108 us (14%)
  starting transfers between devices  56.6 us (7%)
  local copies, waits for them, and re-layouts  48.2 us (6%)
  between operations  41 us (5%)
  matrix products  33.6 us (4%)
    pallas_call x1, Pallas kernels, exchange(): pl.pallas_call(functools.partial(exchange_kernel, grid_size), out_shape=[...  184 us
    ppermute x1, waiting for transfers between devices, on_device(): far_rows = lax.ppermute(near_rows, 'half', swap_half)  171 us
    ppermute x4, starting transfers between devices, on_device(): pieces.append(lax.ppermute(panel, ('row', 'col'), perm))  52.4 us
    another operation x12, other arithmetic, eliminate(): factor = lax.linalg.cholesky(block, symmetrize_input=False)  49.6 us
    another operation x8, other arithmetic, eliminate(): lax.linalg.triangular_solve(factor, identity, left_side=True, lower=True)  41.9 us
    pallas_call x2, Pallas kernels, place(): pl.pallas_call(functools.partial(place_kernel, grid_size, slots, steps),...  41.8 us
    ppermute x4, waiting for transfers between devices, on_device(): pieces.append(lax.ppermute(panel, ('row', 'col'), perm))  40.5 us
    pallas_call x1, Pallas kernels, update(): pl.pallas_call(update_kernel, grid_spec=pltpu.PrefetchScalarGridSpec(num_...  32.3 us
  transfers between devices with their start and end apart: 10, of which 4 were waited for; matrix products, arithmetic and copies ran while one was open for 6% of the time, Pallas kernels for 5%

profile of v3, /device:TPU:18, one launch (start us, length us, event | category | flops | bytes accessed | tf_op | source)
XLA Modules:
  0.0 776.4 jit_solution(6568593051664266442)
XLA Ops:
  40.5 18.7 %shard_map.37.src = f32[4,4,512,512]{3,2,1,0:T(8,128)} custom-call(s32[16]{0:T(128)} %reshape_squeeze.6.row_order, s32[16]{0:T(128)} %reshape_squeeze.7.col_order, f32[2048,2048]{1,0:T(8,128)} %bitcast.161), custom_call_target="tpu_custom_call" | custom-call | tf_op jit(solution)/shard_map/pallas_call | solution.py:38
  59.1 184.1 %shard_map.38 = (f32[4,4,512,512]{3,2,1,0:T(8,128)}, f32[4,4,2,512,512]{4,3,2,1,0:T(8,128)}) custom-call(f32[4,4,512,512]{3,2,1,0:T(8,128)} %shard_map.37.src), custom_call_target="tpu_custom_call" | custom-call | tf_op jit(solution)/shard_map/pallas_call | solution.py:245
  269.9 1.7 collective-permute-start.3
  271.6 46.2 %collective-permute-start.4 = (f32[1280,128]{1,0:T(8,128)}, f32[1280,128]{1,0:T(8,128)S(1)}, u32[]{:S(2)}, u32[]{:S(2)}) collective-permute-start(f32[1280,128]{1,0:T(8,128)} %bitcast.165), channel_id=1, source_target_pairs={{0,4},{1,8},{2,12},{3,0},{4,5},{5,9},{6,13},{7,1},{8,6},{9,10},{10... | collective-permute-start | bytes 1966088 | tf_op jit(solution)/shard_map/ppermute | solution.py:548
  317.8 4.4 collective-permute-start.6
  322.2 8.2 %dynamic-slice_bitcast_fusion = (f32[4,512,512]{2,1,0:T(8,128)}, f32[4,512,512]{2,1,0:T(8,128)}) fusion(f32[4,4,512,512]{3,2,1,0:T(8,128)} %get-tuple-element.114, s32[]{:T(128)S(6)} %select_n.539, s32[]{:T(128)S(6)} %select_n.538), kind=kLoop, calls=%fused_computation.49 | loop fusion | bytes 16777224 | tf_op jit(solution)/shard_map/jit(dynamic_index_in_dim)/squeeze | solution.py:526
  332.6 19.3 %collective-permute-done.4 = f32[1280,128]{1,0:T(8,128)S(1)} collective-permute-done((f32[1280,128]{1,0:T(8,128)}, f32[1280,128]{1,0:T(8,128)S(1)}, u32[]{:S(2)}, u32[]{:S(2)}) %collective-permute-start.4) | collective-permute-done | bytes 655392 | tf_op jit(solution)/shard_map/ppermute | solution.py:548
  351.9 9.9 %collective-permute-done.5 = f32[1280,128]{1,0:T(8,128)S(1)} collective-permute-done((f32[1280,128]{1,0:T(8,128)}, f32[1280,128]{1,0:T(8,128)S(1)}, u32[]{:S(2)}, u32[]{:S(2)}) %collective-permute-start.5) | collective-permute-done | bytes 655392 | tf_op jit(solution)/shard_map/ppermute | solution.py:548
  361.8 11.3 %collective-permute-done.6 = f32[1280,128]{1,0:T(8,128)S(1)} collective-permute-done((f32[1280,128]{1,0:T(8,128)}, f32[1280,128]{1,0:T(8,128)S(1)}, u32[]{:S(2)}, u32[]{:S(2)}) %collective-permute-start.6) | collective-permute-done | bytes 655392 | tf_op jit(solution)/shard_map/ppermute | solution.py:548
  373.3 2.2 gather_fusion.16
  375.5 2.0 select_bitcast_fusion.2
  377.5 5.4 copy.47
  382.9 2.2 reshape.615
  385.8 1.7 slice.110
  388.8 18.9 %shard_map.39.front = f32[1280,2560]{1,0:T(8,128)S(1)} custom-call(s32[8]{0:T(128)S(1)} %add.620.chunk_at, s32[8]{0:T(128)S(1)} %get-tuple-element.139.t_at, s32[16]{0:T(128)S(1)} %and_select_fusion.4.u_at, s32[8]{0:T(128)S(1)} %reshape.618.swapped, s32[2]{0:T(128)S(1)} %convert_element_type.47.valid, f32[1280,2560]{1,0:T(8,128)} %front.1, ...), custom_call_target="tpu_custom_call" | custom-call | flops 4000000000 | bytes 36000000 | tf_op jit(solution)/shard_map/pallas_call | solution.py:330
  407.7 4.9 copy-done
  412.7 170.8 %collective-permute-done.7 = f32[10,128,512]{2,1,0:T(8,128)} collective-permute-done((f32[10,128,512]{2,1,0:T(8,128)}, f32[10,128,512]{2,1,0:T(8,128)}, u32[]{:S(2)}, u32[]{:S(2)}) %collective-permute-start.7) | collective-permute-done | bytes 2621472 | tf_op jit(solution)/shard_map/ppermute | solution.py:552
  583.5 2.1 select_bitcast_fusion.1
  586.3 2.9 copy.48
  589.2 22.9 %shard_map.40.front = f32[1280,2560]{1,0:T(8,128)} custom-call(s32[8]{0:T(128)S(1)} %iota.202.chunk_at, s32[8]{0:T(128)S(1)} %get-tuple-element.141.t_at, s32[16]{0:T(128)S(1)} %and_select_fusion.10.u_at, s32[8]{0:T(128)S(1)} %reshape.617.swapped, s32[2]{0:T(128)S(1)} %convert_element_type.44.valid, f32[1280,2560]{1,0:T(8,128)} %copy-done, ...), custom_call_target="tpu_custom_call" | custom-call | flops 4000000000 | bytes 36000000 | tf_op jit(solution)/shard_map/pallas_call | solution.py:330
  613.4 106.1 %while.16 = (s32[]{:T(128)}, f32[512,512]{1,0:T(8,128)S(1)}, f32[512,512]{1,0:T(8,128)S(1)}, s32[]{:T(128)}, s32[]{:T(128)}, /*index=5*/s32[]{:T(128)}, s32[]{:T(128)}) while((s32[]{:T(128)}, f32[512,512]{1,0:T(8,128)S(1)}, f32[512,512]{1,0:T(8,128)S(1)}, s32[]{:T(128)}, s32[]{:T(128)}, /*index=5*/s32[]{:T(128)}, ...), condition=%wide.region_15.17_spmd.clone, body=%wide.region_12.16_spmd.clone.sunk | while | flops 1032540800 | bytes 7145617 | solution.py:577
  613.6 11.7 %cholesky.73 = f32[128,128]{1,0:T(8,128)S(1)} custom-call(f32[128,128]{1,0:T(8,128)S(1)} %dynamic_slice.154), custom_call_target="Cholesky" | custom-call | tf_op jit(solution)/shard_map/while/body/eval_jaxpr/cholesky | solution.py:564
  626.7 9.8 %custom-call.53 = f32[1,128,128]{1,2,0:T(8,128)S(1)} custom-call(f32[1,128,128]{2,1,0:T(8,128)S(1)} %fusion.134), custom_call_target="InvertDiagBlocksLowerTriangular" | custom-call | tf_op jit(solution)/shard_map/while/body/eval_jaxpr/triangular_solve | solution.py:565
  640.1 11.7 %cholesky.73 = f32[128,128]{1,0:T(8,128)S(1)} custom-call(f32[128,128]{1,0:T(8,128)S(1)} %dynamic_slice.154), custom_call_target="Cholesky" | custom-call | tf_op jit(solution)/shard_map/while/body/eval_jaxpr/cholesky | solution.py:564
  653.1 9.8 %custom-call.53 = f32[1,128,128]{1,2,0:T(8,128)S(1)} custom-call(f32[1,128,128]{2,1,0:T(8,128)S(1)} %fusion.134), custom_call_target="InvertDiagBlocksLowerTriangular" | custom-call | tf_op jit(solution)/shard_map/while/body/eval_jaxpr/triangular_solve | solution.py:565
  666.6 11.7 %cholesky.73 = f32[128,128]{1,0:T(8,128)S(1)} custom-call(f32[128,128]{1,0:T(8,128)S(1)} %dynamic_slice.154), custom_call_target="Cholesky" | custom-call | tf_op jit(solution)/shard_map/while/body/eval_jaxpr/cholesky | solution.py:564
  679.6 9.8 %custom-call.53 = f32[1,128,128]{1,2,0:T(8,128)S(1)} custom-call(f32[1,128,128]{2,1,0:T(8,128)S(1)} %fusion.134), custom_call_target="InvertDiagBlocksLowerTriangular" | custom-call | tf_op jit(solution)/shard_map/while/body/eval_jaxpr/triangular_solve | solution.py:565
  693.0 11.7 %cholesky.73 = f32[128,128]{1,0:T(8,128)S(1)} custom-call(f32[128,128]{1,0:T(8,128)S(1)} %dynamic_slice.154), custom_call_target="Cholesky" | custom-call | tf_op jit(solution)/shard_map/while/body/eval_jaxpr/cholesky | solution.py:564
  706.1 9.8 %custom-call.53 = f32[1,128,128]{1,2,0:T(8,128)S(1)} custom-call(f32[1,128,128]{2,1,0:T(8,128)S(1)} %fusion.134), custom_call_target="InvertDiagBlocksLowerTriangular" | custom-call | tf_op jit(solution)/shard_map/while/body/eval_jaxpr/triangular_solve | solution.py:565
  719.5 12.8 %and_select_fusion.lcol = f32[2560,512]{1,0:T(8,128)} fusion(f32[2560,512]{1,0:T(8,128)} %bitcast.160, f32[512,512]{1,0:T(8,128)S(1)} %get-tuple-element.120, pred[512]{0:T(512)(128)(4,1)S(1)} %iota_compare_fusion.14, pred[2560]{0:T(1024)(128)(4,1)S(1)} %fusion.57), kind=kOutput, calls=%fused_computation.48 | convolution fusion | flops 8055685120 | bytes 11537408 | tf_op jit(solution)/shard_map/dot_general | solution.py:580
  732.3 4.5 convolution_select_fusion.1.lrow
  736.8 32.3 %shard_map.41 = f32[1280,2560]{1,0:T(8,128)} custom-call(s32[2]{0:T(128)S(1)} %pad_add_fusion.place_of, f32[1280,2560]{1,0:T(8,128)} %shard_map.40.front, f32[1280,512]{1,0:T(8,128)S(1)} %convolution_select_fusion.1.lrow, f32[2560,512]{1,0:T(8,128)} %and_select_fusion.lcol), custom_call_target="tpu_custom_call" | custom-call | flops 10000000000 | bytes 34000000 | tf_op jit(solution)/shard_map/pallas_call | solution.py:394
  (215 shorter events, 59.2 us)
Async XLA Ops:
  6.5 379.2 %all-gather.3.cloned.1.call-start = ((), (), s32[]{:S(2)}) async-start(), calls=%async_computation | async-start | bytes 3276800 | tf_op jit(solution)/shard_map/all_gather | solution.py:539
  244.8 4.6 copy-start.3
  247.8 19.4 %collective-permute-start.2 = (f32[2,512,128]{2,1,0:T(8,128)S(1)}, f32[2,512,128]{2,1,0:T(8,128)S(1)}, u32[]{:S(2)}, u32[]{:S(2)}) collective-permute-start(f32[2,512,128]{2,1,0:T(8,128)S(1)} %maximum_select_fusion.2), channel_id=1, source_target_pairs={{0,16},{16,0},{1,17},{17,1},{2,18},{18,2},{3,19},{19,3},{4,20},{20... | collective-permute-start | bytes 1572872 | tf_op jit(solution)/shard_map/ppermute | solution.py:523
  265.8 2.8 slice-start
  269.8 342.3 %all-gather.5.cloned.1.call-start = ((), (), s32[]{:S(2)}) async-start(), calls=%async_computation.1 | async-start | bytes 2359296 | tf_op jit(solution)/shard_map/all_gather | solution.py:540
  269.9 61.3 %collective-permute-start.3 = (f32[1280,128]{1,0:T(8,128)}, f32[1280,128]{1,0:T(8,128)S(1)}, u32[]{:S(2)}, u32[]{:S(2)}) collective-permute-start(f32[1280,128]{1,0:T(8,128)} %bitcast.164), channel_id=1, source_target_pairs={{0,0},{1,4},{2,8},{3,12},{4,1},{5,5},{6,9},{7,13},{8,2},{9,6},{10,... | collective-permute-start | bytes 1966088 | tf_op jit(solution)/shard_map/ppermute | solution.py:548
  271.6 80.3 %collective-permute-start.4 = (f32[1280,128]{1,0:T(8,128)}, f32[1280,128]{1,0:T(8,128)S(1)}, u32[]{:S(2)}, u32[]{:S(2)}) collective-permute-start(f32[1280,128]{1,0:T(8,128)} %bitcast.165), channel_id=1, source_target_pairs={{0,4},{1,8},{2,12},{3,0},{4,5},{5,9},{6,13},{7,1},{8,6},{9,10},{10... | collective-permute-start | bytes 1966088 | tf_op jit(solution)/shard_map/ppermute | solution.py:548
  317.8 44.0 %collective-permute-start.5 = (f32[1280,128]{1,0:T(8,128)}, f32[1280,128]{1,0:T(8,128)S(1)}, u32[]{:S(2)}, u32[]{:S(2)}) collective-permute-start(f32[1280,128]{1,0:T(8,128)} %bitcast.166), channel_id=1, source_target_pairs={{0,8},{1,12},{2,0},{3,4},{4,9},{5,13},{6,1},{7,5},{8,10},{9,14},{1... | collective-permute-start | bytes 1966088 | tf_op jit(solution)/shard_map/ppermute | solution.py:548
  317.8 55.3 %collective-permute-start.6 = (f32[1280,128]{1,0:T(8,128)}, f32[1280,128]{1,0:T(8,128)S(1)}, u32[]{:S(2)}, u32[]{:S(2)}) collective-permute-start(f32[1280,128]{1,0:T(8,128)} %bitcast.167), channel_id=1, source_target_pairs={{0,12},{1,0},{2,4},{3,8},{4,13},{5,1},{6,5},{7,9},{8,14},{9,2},{10... | collective-permute-start | bytes 1966088 | tf_op jit(solution)/shard_map/ppermute | solution.py:548
  330.5 258.7 %collective-permute-start = (f32[4,512,512]{2,1,0:T(8,128)}, f32[4,512,512]{2,1,0:T(8,128)}, u32[]{:S(2)}, u32[]{:S(2)}) collective-permute-start(f32[4,512,512]{2,1,0:T(8,128)} %get-tuple-element.157), channel_id=1, source_target_pairs={{0,16},{16,0},{1,17},{17,1},{2,18},{18,2},{3,19},{19,3},{4,20},{20... | collective-permute-start | bytes 12582920 | tf_op jit(solution)/shard_map/ppermute | solution.py:525
  331.1 258.0 %collective-permute-start.1 = (f32[4,512,512]{2,1,0:T(8,128)}, f32[4,512,512]{2,1,0:T(8,128)}, u32[]{:S(2)}, u32[]{:S(2)}) collective-permute-start(f32[4,512,512]{2,1,0:T(8,128)} %get-tuple-element.156), channel_id=1, source_target_pairs={{0,16},{16,0},{1,17},{17,1},{2,18},{18,2},{3,19},{19,3},{4,20},{20... | collective-permute-start | bytes 12582920 | tf_op jit(solution)/shard_map/ppermute | solution.py:525
  385.1 198.4 %collective-permute-start.7 = (f32[10,128,512]{2,1,0:T(8,128)}, f32[10,128,512]{2,1,0:T(8,128)}, u32[]{:S(2)}, u32[]{:S(2)}) collective-permute-start(f32[10,128,512]{2,1,0:T(8,128)} %reshape.615), channel_id=1, source_target_pairs={{0,16},{16,0},{1,17},{17,1},{2,18},{18,2},{3,19},{19,3},{4,20},{20... | collective-permute-start | bytes 7864328 | tf_op jit(solution)/shard_map/ppermute | solution.py:552
  388.8 194.7 %copy-start.1 = (f32[10,128,512]{2,1,0:T(8,128)S(1)}, f32[10,128,512]{2,1,0:T(8,128)}, u32[]{:S(2)}) copy-start(f32[10,128,512]{2,1,0:T(8,128)} %reshape.615) | copy-start | bytes 7864324
  407.7 5.0 copy-start
  719.5 12.8 %copy-start.2 = (f32[1280,512]{1,0:T(8,128)S(1)}, f32[1280,512]{1,0:T(8,128)}, u32[]{:S(2)}) copy-start(f32[1280,512]{1,0:T(8,128)} %all-gather.3.cloned.1.call-done) | copy-start | bytes 7864324
Sparse Core Ops, SparseCore 0:
  269.9 94.3 all-gather.2
  387.6 66.6 all-gather.4
